TPU v7x, 256 devices: a whole 4x4x8 slice. The times are simulated.
256 devices in a mesh: gx: 4 (over x), gy: 8 (over z), gz: 8 (over y, core).
Axes of the slice: x: 4, y: 4, z: 8, core: 2. Of those that a mesh axis runs over, the one named last changes fastest.
Arguments:
- nodal_field: float32 [128, 1024, 2048], P('gx', 'gy', 'gz'), may hold values from -6 to 6
- spacing_x: float32 [128], replicated, may hold values from 0.5 to 2
- spacing_z: float32 [2048], replicated, may hold values from 0.5 to 2
- operator_x: float32 [64, 16], P('gx'), may hold values from -1.5 to 1.5
- persist_x: float32 [64], P('gx'), may hold values from 0.6 to 1
- operator_z: float32 [1024, 128], P('gz'), may hold values from -0.5 to 0.5
- persist_z: float32 [1024], P('gz'), may hold values from 0.6 to 1
- receivers: int32 [131072, 1], P(('gx', 'gy', 'gz')), may hold values from 0 to 63; in each aligned block of 512 rows (0 to 511, 512 to 1023, ...) at most 16 rows name the same one
Outputs:
- detail_x: float32 [64, 1024, 2048], P('gx', 'gy', 'gz')
- detail_z: float32 [64, 1024, 1024], P('gx', 'gy', 'gz')
- received: float32 [256, 64, 16, 2, 4, 128], P(('gx', 'gy', 'gz'))
Inputs may be any that keep to these rules, and one draw needn't show every extreme that they name: `receivers`: each row names the receiving device of one kept block among the 64 devices with the same gx index, in (gy, gz) row-major order; of the 512 blocks of one device at most 16 name the same receiver, and that bound is reached.
All inputs are finite; a program needn't handle non-finite values.
Results may differ from a plain program's by a relative error of at most 0.00008.
Values sent between devices are 32-bit elements; how exact they have to be, the bound alone decides.
No kernel may reach another device: no remote copies, remote signals or barrier semaphores. Data moves between devices by JAX's collectives and lax.ppermute only.
A program may use at most 64 MiB of HBM per device.

v0:
```python
import jax
import jax.numpy as jnp
from jax import lax
from jax.sharding import PartitionSpec as P

LINES = 4


def extended(block, sides, width):
    for axis, dim in sides:
        count = lax.axis_size(axis)
        forward = [(i, i + 1) for i in range(count - 1)]
        backward = [(target, source) for source, target in forward]
        low = lax.ppermute(
            lax.slice_in_dim(block, block.shape[dim] - width, None, axis=dim), axis, forward
        )
        high = lax.ppermute(lax.slice_in_dim(block, 0, width, axis=dim), axis, backward)
        block = jnp.concatenate([low, block, high], axis=dim)
    return block


def carried_in(array, axis, combine, identity):
    size, index = (lax.axis_size(axis), lax.axis_index(axis))
    everything = jax.tree.map(lambda part: lax.all_gather(part, axis), array)
    start = jax.tree.map(
        lambda part, zero: jnp.broadcast_to(jnp.asarray(zero, part.dtype), part.shape),
        array,
        identity,
    )

    def step(k, before):
        reached = k < index
        new = combine(before, jax.tree.map(lambda part: part[k], everything))
        return jax.tree.map(lambda a, b: jnp.where(reached, a, b), new, before)

    return lax.fori_loop(0, size, step, start)


def compose(earlier, later):
    return (earlier[0] * later[0], later[1] + later[0] * earlier[1])


def edges_first(border):
    return extended(border, (("gx", 0),), 2)


def edges_third(border):
    return extended(border, (("gz", 2),), 2)


def chain_first(gain_end, value_end):
    identity = (jnp.ones_like(gain_end), jnp.zeros_like(value_end))
    return carried_in((gain_end, value_end), "gx", compose, identity)[1]


def chain_third(gain_end, value_end):
    identity = (jnp.ones_like(gain_end), jnp.zeros_like(value_end))
    return carried_in((gain_end, value_end), "gz", compose, identity)[1]


def expand(vector, direction):
    shape_list = [1, 1, 1]
    shape_list[direction] = -1
    return vector.reshape(shape_list)


def refine(nodes, spacing, row_blocks, gain_list, direction, device_rank, edges_move, chain_move):
    length = nodes.shape[direction]
    coarse_count = length // 2
    offset = device_rank * length
    local_space = lax.dynamic_slice_in_dim(spacing, offset, length)
    prev_space = lax.dynamic_slice_in_dim(spacing, jnp.maximum(offset - 2, 0), 2)
    space_even = local_space[0::2]
    space_odd = local_space[1::2]
    span_sum = space_even + space_odd
    weight_a = space_odd / span_sum
    weight_b = space_even / span_sum
    even_nodes = lax.slice_in_dim(nodes, 0, length, 2, direction)
    odd_nodes = lax.slice_in_dim(nodes, 1, length, 2, direction)
    border = jnp.concatenate(
        [
            lax.slice_in_dim(nodes, 0, 2, axis=direction),
            lax.slice_in_dim(nodes, length - 2, length, axis=direction),
        ],
        direction,
    )
    widened = edges_move(border)
    left_even = lax.slice_in_dim(widened, 0, 1, axis=direction)
    left_odd = lax.slice_in_dim(widened, 1, 2, axis=direction)
    beyond = lax.slice_in_dim(widened, 6, 7, axis=direction)
    right_nodes = jnp.concatenate(
        [lax.slice_in_dim(even_nodes, 1, coarse_count, axis=direction), beyond], direction
    )
    detail = (
        odd_nodes
        - expand(weight_a, direction) * even_nodes
        - expand(weight_b, direction) * right_nodes
    )
    first_even = lax.slice_in_dim(even_nodes, 0, 1, axis=direction)
    prev_sum = prev_space[0] + prev_space[1]
    left_detail = (
        left_odd - prev_space[1] / prev_sum * left_even - prev_space[0] / prev_sum * first_even
    )
    from_left = jnp.where(device_rank > 0, 0.5 * prev_space[1] * left_detail, 0.0)
    near_terms = 0.5 * expand(space_even, direction) * detail
    far_terms = 0.5 * expand(space_odd, direction) * detail
    load_terms = near_terms + jnp.concatenate(
        [from_left, lax.slice_in_dim(far_terms, 0, coarse_count - 1, axis=direction)], direction
    )
    if direction == 0:
        local_part = jnp.einsum(
            "ij,jab->iab", row_blocks, load_terms, precision=lax.Precision.HIGHEST
        )
    else:
        local_part = jnp.einsum(
            "ij,abj->abi", row_blocks, load_terms, precision=lax.Precision.HIGHEST
        )
    tail_values = lax.slice_in_dim(local_part, coarse_count - 1, coarse_count, axis=direction)
    gain_end = gain_list[coarse_count - 1 : coarse_count].reshape(1, 1, 1)
    carried = chain_move(gain_end, tail_values)
    solved = local_part + expand(gain_list, direction) * carried
    return (detail, even_nodes + solved)


def local(
    nodal_field, spacing_x, spacing_z, operator_x, persist_x, operator_z, persist_z, receivers
):
    index_first = lax.axis_index("gx")
    index_third = lax.axis_index("gz")
    detail_x, coarse_x = refine(
        nodal_field, spacing_x, operator_x, persist_x, 0, index_first, edges_first, chain_first
    )
    detail_z, coarse_z = refine(
        coarse_x, spacing_z, operator_z, persist_z, 2, index_third, edges_third, chain_third
    )
    depth_cells = coarse_z.shape[2]
    block_count = coarse_z.shape[0] * coarse_z.shape[1] // LINES
    tile_rows = jnp.stack(
        [
            coarse_z.reshape(block_count, LINES, depth_cells),
            detail_z.reshape(block_count, LINES, depth_cells),
        ],
        1,
    )
    tile_rows = tile_rows.reshape(block_count, 2 * LINES * depth_cells)
    group_size = lax.axis_size("gy") * lax.axis_size("gz")
    capacity = max(2, block_count // group_size * 2)
    targets = receivers[:, 0]
    positions = jnp.arange(block_count, dtype=jnp.int32)
    earlier = (targets[None, :] == targets[:, None]) & (positions[None, :] < positions[:, None])
    slots = jnp.sum(earlier.astype(jnp.int32), axis=1)
    placed = targets * capacity + slots
    selector = (
        placed[None, :] == jnp.arange(group_size * capacity, dtype=jnp.int32)[:, None]
    ).astype(jnp.float32)
    outgoing = jnp.dot(
        selector, tile_rows, precision=lax.Precision.HIGHEST, preferred_element_type=jnp.float32
    )
    outgoing = outgoing.reshape(group_size, capacity, 2 * LINES * depth_cells)
    incoming = lax.all_to_all(outgoing, ("gy", "gz"), split_axis=0, concat_axis=0, tiled=True)
    received = incoming.reshape(1, group_size, capacity, 2, LINES, depth_cells)
    return (detail_x, detail_z, received)


def solution(mesh):
    return jax.shard_map(
        local,
        mesh=mesh,
        in_specs=(
            P("gx", "gy", "gz"),
            P(),
            P(),
            P("gx", None),
            P("gx"),
            P("gz", None),
            P("gz"),
            P(("gx", "gy", "gz"), None),
        ),
        out_specs=(
            P("gx", "gy", "gz"),
            P("gx", "gy", "gz"),
            P(("gx", "gy", "gz"), None, None, None, None, None),
        ),
        check_vma=False,
    )
```

profile of v0, /device:TPU:8, one launch (start us, length us, event | category | flops | bytes accessed | tf_op | source)
XLA Modules:
  0.0 247.4 jit_solution(8754598489175844673)
XLA Ops:
  1.9 1.3 collective-permute-start
  3.4 4.6 %collective-permute-start.1 = (f32[2,128,256]{1,0,2:T(2,128)S(1)}, f32[2,128,256]{1,0,2:T(2,128)S(1)}, u32[]{:S(2)}, u32[]{:S(2)}) collective-permute-start(f32[2,128,256]{1,0,2:T(2,128)S(1)} %copy.111), channel_id=1, source_target_pairs={{0,64},{64,128},{128,192},{1,65},{65,129},{129,193},{2,66},{66,130... | collective-permute-start | bytes 786440 | tf_op jit(solution)/shard_map/ppermute | solution.py:14
  9.5 4.0 %fusion.26 = (f32[16,128,256]{2,1,0:T(8,128)S(1)}, f32[16,128,256]{2,1,0:T(8,128)}) fusion(f32[32,128,256]{2,1,0:T(8,128)} %param.12), kind=kLoop, calls=%fused_computation.60 | loop fusion | bytes 8388608 | tf_op jit(solution)/shard_map/slice | solution.py:79
  17.3 9.3 %all-reduce = f32[4]{0:T(128)S(1)} all-reduce(f32[4]{0:T(128)S(1)} %slice_dynamic-update-slice_fusion.1), channel_id=3, replica_groups=mesh['gx'=4,'gy'=8,'gz'=8] {'gx'}, use_global_device_ids=true, to_apply=%add | all-reduce | flops 4 | bytes 32
  30.6 2.0 copy.108
  32.6 2.2 copy.109
  38.4 2.3 fusion.8
  40.7 1.3 copy-done.5
  42.2 12.8 %all-gather = f32[4,128,256]{2,1,0:T(8,128)S(1)} all-gather(f32[1,128,256]{2,1,0:T(8,128)S(1)} %copy.94), channel_id=2, replica_groups=mesh['gx'=4,'gy'=8,'gz'=8] {'gx'}, dimensions={0}, use_global_device_ids=true | all-gather | bytes 655360 | tf_op jit(solution)/shard_map/all_gather | solution.py:24
  55.0 5.4 %while.28 = (s32[]{:T(128)}, f32[1,128,256]{2,1,0:T(8,128)S(1)}, s32[]{:T(128)}, f32[4,1,128,256]{3,2,1,0:T(8,128)S(1)}, f32[4,1,1,1]{0,3,2,1:T(1,128)S(1)}, /*index=5*/s32[]{:T(128)}, s32[]{:T(128)}) while((s32[]{:T(128)}, f32[1,128,256]{2,1,0:T(8,128)S(1)}, s32[]{:T(128)}, f32[4,1,128,256]{3,2,1,0:T(8,128)S(1)}, ...), condition=%wide.region_1.2_spmd.clone, body=%wide.region_0.1_spmd.clone.sunk | while | flops 131076 | bytes 393341 | solution.py:36
  60.5 2.0 add_add_fusion
  62.5 1.3 copy-done.3
  63.8 1.9 collective-permute-start.2
  66.3 12.5 %all-reduce.1 = f32[8]{0:T(128)S(1)} all-reduce(f32[8]{0:T(128)S(1)} %slice_dynamic-update-slice_fusion), channel_id=5, replica_groups=mesh['gx'=4,'gy'=8,'gz'=8] {'gz'}, use_global_device_ids=true, to_apply=%add.1 | all-reduce | flops 8 | bytes 64
  82.0 1.5 slice.121
  83.5 1.9 collective-permute-start.3
  87.1 1.4 copy.105
  89.3 1.4 maximum_add_fusion.4
  90.7 1.9 fusion.10
  92.6 1.4 copy.100
  94.0 1.3 slice.151
  95.3 1.6 copy.98
  97.0 12.9 %all-gather.2 = f32[128,128,1]{1,2,0:T(1,128)S(1)} all-gather(f32[16,128,1]{1,2,0:T(1,128)S(1)} %copy.98), channel_id=4, replica_groups=mesh['gx'=4,'gy'=8,'gz'=8] {'gz'}, dimensions={0}, use_global_device_ids=true | all-gather | bytes 73728 | tf_op jit(solution)/shard_map/all_gather | solution.py:24
  109.9 10.5 %while.29 = (s32[]{:T(128)}, f32[16,128,1]{1,2,0:T(1,128)S(1)}, s32[]{:T(128)}, f32[8,16,128,1]{2,1,3,0:T(8,128)S(1)}, f32[8,1,1,1]{0,3,2,1:T(1,128)S(1)}, /*index=5*/s32[]{:T(128)}, s32[]{:T(128)}) while((s32[]{:T(128)}, f32[16,128,1]{1,2,0:T(1,128)S(1)}, s32[]{:T(128)}, f32[8,16,128,1]{2,1,3,0:T(8,128)S(1)}, ...), condition=%wide.region_4.5_spmd.clone, body=%wide.region_3.4_spmd.clone.sunk | while | flops 8196 | bytes 41085 | solution.py:36
  121.6 1.7 copy.101
  123.8 1.7 copy.103
  125.5 2.1 reshape.92
  127.6 5.1 %fusion.6 = f32[64,16,1024]{2,1,0:T(8,128)} fusion(f32[512,1024,1]{1,0,2:T(8,128)S(1)} %reshape.92, s32[64,16]{1,0:T(8,128)S(1)} %multiply_add_fusion, s32[512]{0:T(512)S(1)} %multiply_add_fusion.1), kind=kOutput, calls=%fused_computation.17 | convolution fusion | flops 6442975232 | bytes 6297600 | tf_op jit(solution)/shard_map/dot_general | solution.py:156
  132.7 13.0 %all-to-all-start = ((f32[64,16,1024]{2,1,0:T(8,128)}), f32[64,16,1024]{2,1,0:T(8,128)}, u32[]{:S(2)}, u32[]{:S(2)}) async-start(f32[64,16,1024]{2,1,0:T(8,128)} %fusion.6), calls=%async_computation | async-start | bytes 8388608 | tf_op jit(solution)/shard_map/all_to_all | solution.py:160
  145.7 1.8 copy.104
  147.5 94.3 %all-to-all-done = f32[64,16,1024]{2,1,0:T(8,128)} async-done(((f32[64,16,1024]{2,1,0:T(8,128)}), f32[64,16,1024]{2,1,0:T(8,128)}, u32[]{:S(2)}, u32[]{:S(2)}) %all-to-all-start) | async-done | bytes 4194336 | tf_op jit(solution)/shard_map/all_to_all | solution.py:160
  241.8 5.6 %reshape.75 = f32[1,64,16,2,4,128]{5,4,3,2,1,0:T(4,128)} reshape(f32[64,16,1024]{2,1,0:T(8,128)} %all-to-all-done) | data formatting | bytes 8388608 | tf_op jit(solution)/shard_map/reshape | solution.py:161
  (110 shorter events, 31.6 us)
Async XLA Ops:
  0.6 90.1 %copy-start = (f32[128,128]{1,0:T(8,128)S(1)}, f32[128,128]{1,0:T(8,128)}, u32[]{:S(2)}) copy-start(f32[128,128]{1,0:T(8,128)} %param.17) | copy-start | bytes 196612
  0.6 8.5 %copy-start.14 = (f32[128]{0:T(128)S(1)}, f32[128]{0:T(128)}, u32[]{:S(2)}) copy-start(f32[128]{0:T(128)} %param.13) | copy-start | bytes 1540
  1.9 33.2 %collective-permute-start = (f32[2,128,256]{1,0,2:T(2,128)S(1)}, f32[2,128,256]{1,0,2:T(2,128)}, u32[]{:S(2)}, u32[]{:S(2)}) collective-permute-start(f32[2,128,256]{1,0,2:T(2,128)S(1)} %copy.110), channel_id=1, source_target_pairs={{64,0},{128,64},{192,128},{65,1},{129,65},{193,129},{66,2},{130,66... | collective-permute-start | bytes 786440 | tf_op jit(solution)/shard_map/ppermute | solution.py:17
  3.4 34.0 %collective-permute-start.1 = (f32[2,128,256]{1,0,2:T(2,128)S(1)}, f32[2,128,256]{1,0,2:T(2,128)S(1)}, u32[]{:S(2)}, u32[]{:S(2)}) collective-permute-start(f32[2,128,256]{1,0,2:T(2,128)S(1)} %copy.111), channel_id=1, source_target_pairs={{0,64},{64,128},{128,192},{1,65},{65,129},{129,193},{2,66},{66,130... | collective-permute-start | bytes 786440 | tf_op jit(solution)/shard_map/ppermute | solution.py:14
  9.5 4.1 %copy-start.16 = (u32[256]{0:T(256)S(1)}, u32[256]{0:T(256)}, u32[]{:S(2)}) copy-start(u32[256]{0:T(256)} %constant.88) | copy-start | bytes 3076
  9.5 4.7 %copy-start.15 = (u32[256]{0:T(256)S(1)}, u32[256]{0:T(256)}, u32[]{:S(2)}) copy-start(u32[256]{0:T(256)} %constant.83) | copy-start | bytes 3076
  9.5 5.9 %copy-start.10 = (s32[512,1]{0,1:T(1,128)S(1)}, s32[512,1]{0,1:T(1,128)}, u32[]{:S(2)}) copy-start(s32[512,1]{0,1:T(1,128)} %param.19) | copy-start | bytes 6148
  9.5 6.2 %copy-start.12 = (f32[16]{0:T(128)S(1)}, f32[16]{0:T(128)}, u32[]{:S(2)}) copy-start(f32[16]{0:T(128)} %param.16) | copy-start | bytes 196
  9.5 7.0 %copy-start.13 = (f32[128]{0:T(128)S(1)}, f32[128]{0:T(128)}, u32[]{:S(2)}) copy-start(f32[128]{0:T(128)} %param.18) | copy-start | bytes 1540
  34.8 1.7 copy-start.6
  37.1 1.3 copy-start.1
  37.1 1.3 copy-start.11
  40.7 1.3 copy-start.5
  62.5 1.3 copy-start.3
  63.8 21.7 %collective-permute-start.2 = (f32[16,128,2]{1,0,2:T(8,128)S(1)}, f32[16,128,2]{1,0,2:T(8,128)S(1)}, u32[]{:S(2)}, u32[]{:S(2)}) collective-permute-start(f32[16,128,2]{1,0,2:T(8,128)S(1)} %get-tuple-element.319), channel_id=1, source_target_pairs={{1,0},{2,1},{3,2},{4,3},{5,4},{6,5},{7,6},{9,8},{10,9},{11,10},{12... | collective-permute-start | bytes 49160 | tf_op jit(solution)/shard_map/ppermute | solution.py:17
  82.0 3.5 %copy-start.4 = (f32[16,128,256]{1,0,2:T(8,128)S(1)}, f32[16,128,256]{1,0,2:T(8,128)}, u32[]{:S(2)}) copy-start(f32[16,128,256]{1,0,2:T(8,128)} %copy-done.3) | copy-start | bytes 6291460
  83.5 2.0 copy-start.8
  83.5 5.1 %collective-permute-start.3 = (f32[16,128,2]{1,0,2:T(8,128)S(1)}, f32[16,128,2]{1,0,2:T(8,128)S(1)}, u32[]{:S(2)}, u32[]{:S(2)}) collective-permute-start(f32[16,128,2]{1,0,2:T(8,128)S(1)} %get-tuple-element.318), channel_id=1, source_target_pairs={{0,1},{1,2},{2,3},{3,4},{4,5},{5,6},{6,7},{8,9},{9,10},{10,11},{11... | collective-permute-start | bytes 49160 | tf_op jit(solution)/shard_map/ppermute | solution.py:14
  95.3 25.1 %copy-start.7 = (f32[16,128,128]{1,0,2:T(8,128)S(1)}, f32[16,128,128]{1,0,2:T(8,128)}, u32[]{:S(2)}) copy-start(f32[16,128,128]{1,0,2:T(8,128)} %copy.100) | copy-start | bytes 3145732
  121.6 1.7 copy-start.9
  132.7 13.0 %copy-start.2 = (f32[16,128,256]{1,0,2:T(8,128)S(1)}, f32[16,128,256]{1,0,2:T(8,128)}, u32[]{:S(2)}) copy-start(f32[16,128,256]{1,0,2:T(8,128)} %copy-done.1) | copy-start | bytes 6291460
  132.7 109.1 %all-to-all-start = ((f32[64,16,1024]{2,1,0:T(8,128)}), f32[64,16,1024]{2,1,0:T(8,128)}, u32[]{:S(2)}, u32[]{:S(2)}) async-start(f32[64,16,1024]{2,1,0:T(8,128)} %fusion.6), calls=%async_computation | async-start | bytes 8388608 | tf_op jit(solution)/shard_map/all_to_all | solution.py:160
where the time goes:
time: 248 us; the launch traced here: 247 us
  waiting for transfers between devices  94.4 us (38%)
  local copies, waits for them, and re-layouts  49.3 us (20%)
  blocking collectives  47.5 us (19%)
  starting transfers between devices  22.7 us (9%)
  other arithmetic  16.5 us (7%)
  matrix products  9.33 us (4%)
  between operations  7.52 us (3%)
    all_to_all x1, waiting for transfers between devices, local(): lax.all_to_all(outgoing, ('gy', 'gz'), split_axis=0, concat_axis=0, tiled...  94.3 us
    all_gather x2, blocking collectives, carried_in(): everything = jax.tree.map(lambda part: lax.all_gather(part, axis), array)  25.7 us
    unnamed x2, blocking collectives  21.8 us
    unnamed x46, local copies, waits for them, and re-layouts  14.3 us
    all_to_all x1, starting transfers between devices, local(): lax.all_to_all(outgoing, ('gy', 'gz'), split_axis=0, concat_axis=0, tiled...  13 us
    select_n x12, other arithmetic, step(): return jax.tree.map(lambda a, b: jnp.where(reached, a, b), new, before)  7.88 us
    dynamic_slice x20, local copies, waits for them, and re-layouts, step(): new = combine(before, jax.tree.map(lambda part: part[k], everything))  7.79 us
    ppermute x2, starting transfers between devices, extended(): lax.ppermute(lax.slice_in_dim(block, block.shape[dim] - width, None, axis...  6.48 us
  transfers between devices with their start and end apart: 5, of which 2 were waited for; matrix products, arithmetic and copies ran while one was open for 9% of the time, Pallas kernels for 0%

commit v1 on v0

v1 whole, which is shorter than its diff:
```python
import jax
import jax.numpy as jnp
from jax import lax
from jax.experimental import pallas as pl
from jax.experimental.pallas import tpu as pltpu
from jax.sharding import PartitionSpec as P

LINES = 4
F32 = jnp.float32
BF16 = jnp.bfloat16
SMEM = pltpu.SMEM
VMEM = pltpu.VMEM
LIMIT = 48 * 1024 * 1024


def spec(space):
    return pl.BlockSpec(memory_space=space)


def cost(flops, moved):
    return pl.CostEstimate(flops=flops, bytes_accessed=moved, transcendentals=0)


def params():
    return pltpu.CompilerParams(vmem_limit_bytes=LIMIT)


def ratio(top, bottom):
    return jnp.full((1, 1), top, F32) / jnp.full((1, 1), bottom, F32)


def weights_x(rank_ref, h_ref, k):
    base = rank_ref[0] * 32 + 2 * k
    if k < 0:
        base = jnp.maximum(base, 0)
    even, odd = h_ref[base], h_ref[base + 1]
    total = even + odd
    near, far = 0.5 * even, 0.5 * odd
    if k < 0:
        far = jnp.where(rank_ref[0] > 0, far, 0.0)
    return ratio(odd, total), ratio(even, total), near, far


def edge_kernel(rank_ref, h_ref, low_ref, high_ref, first_ref, last_ref):
    a, _, _, _ = weights_x(rank_ref, h_ref, 15)
    first_ref[...] = low_ref[0]
    last_ref[...] = high_ref[1] - a * high_ref[0]


def tail_kernel(rank_ref, h_ref, f_ref, x_ref, out_ref):
    _, b_before, _, far_before = weights_x(rank_ref, h_ref, -1)
    before = -f_ref[15, 0] * far_before * b_before
    total = None
    for j in range(16):
        a, b, near, far = weights_x(rank_ref, h_ref, j)
        v = f_ref[15, j] * near
        if j < 15:
            v = v + f_ref[15, j + 1] * far
        term = (before - v * a) * x_ref[2 * j] + v * x_ref[2 * j + 1]
        total = term if total is None else total + term
        before = -v * b
    out_ref[...] = total


def close_kernel(rank_ref, h_ref, f_ref, g_ref, own_ref, right_ref, left_ref, out_ref):
    _, b, near, _ = weights_x(rank_ref, h_ref, 15)
    _, _, _, far = weights_x(rank_ref, h_ref, -1)
    alpha = -(f_ref[15, 15] * near) * b
    beta = f_ref[15, 0] * far
    out_ref[0:128, :] = own_ref[...] + alpha * right_ref[...] + beta * left_ref[...]
    out_ref[128:136, :] = jnp.full((8, 256), g_ref[15], F32)


def split(value):
    high = value.astype(BF16)
    return high, (value - high.astype(F32)).astype(BF16)


def dot3(value, high, low):
    v_high, v_low = split(value)
    one = lambda a, b: jnp.dot(a, b, preferred_element_type=F32)
    return one(v_high, high) + (one(v_low, high) + one(v_high, low))


def table_kernel(rank_ref, h_ref, even_ref, odd_ref, f_ref, g_ref, high_ref, low_ref, row_ref):
    even, odd = even_ref[...], odd_ref[...]
    total = even + odd
    a, b = odd / total, even / total
    near, far = 0.5 * even, 0.5 * odd
    at = jnp.maximum(rank_ref[0] * 256 - 2, 0)
    h_even, h_odd = h_ref[at], h_ref[at + 1]
    far_before = jnp.where(rank_ref[0] > 0, 0.5 * h_odd, 0.0)
    b_before = ratio(h_even, h_even + h_odd)
    z = lax.broadcasted_iota(jnp.int32, (256, 128), 0)
    k = lax.broadcasted_iota(jnp.int32, (256, 128), 1)
    chosen = jnp.where(z == 2 * k, 1.0, 0.0)
    detail = jnp.where(z == 2 * k + 1, 1.0, 0.0) - chosen * a - jnp.where(z == 2 * k + 2, b, 0.0)
    shifted = jnp.where(k == 0, 0.0, pltpu.roll(detail * far, 1, 1))
    load = detail * near + shifted
    load = load - jnp.where((z == 0) & (k == 0), far_before * b_before, 0.0)
    contract = (((1,), (1,)), ((), ()))
    coarse = chosen + lax.dot_general(
        load, f_ref[...], contract, precision=lax.Precision.HIGHEST, preferred_element_type=F32
    )
    high, low = split(detail)
    high_ref[:, 0:128], low_ref[:, 0:128] = high, low
    high, low = split(coarse)
    high_ref[:, 128:256], low_ref[:, 128:256] = high, low
    row = lax.broadcasted_iota(jnp.int32, (8, 128), 0)
    lane = lax.broadcasted_iota(jnp.int32, (8, 128), 1)
    pick = jnp.where(((row == 1) & (lane == 127)) | ((row == 2) & (lane == 0)), 1.0, 0.0)
    columns = lax.dot_general(
        pick, f_ref[...], contract, precision=lax.Precision.HIGHEST, preferred_element_type=F32
    )
    last = lane[0:1] == 127
    b_last = jnp.sum(jnp.where(last, b, 0.0), axis=1, keepdims=True)
    near_last = jnp.sum(jnp.where(last, near, 0.0), axis=1, keepdims=True)
    end = lambda v: jnp.broadcast_to(jnp.sum(jnp.where(last, v, 0.0), axis=1, keepdims=True), (1, 128))
    from_right = columns[1:2] * (-near_last * b_last)
    from_left = columns[2:3] * far_before
    gain = g_ref[...]
    row_ref[0:1] = jnp.where(last, -b, 0.0)
    row_ref[1:2] = from_right
    row_ref[2:3] = from_left
    row_ref[3:4] = gain
    row_ref[4:5] = end(from_right)
    row_ref[5:6] = end(from_left)
    row_ref[6:7] = end(gain)
    row_ref[7:8] = jnp.zeros((1, 128), F32)


def main_kernel(
    rank_ref, h_ref, f_ref, x_ref, right_ref, left_ref, high_ref, low_ref,
    detail_ref, dz_ref, cz_ref, column_ref, w_ref, v_ref,
):
    @pl.when(pl.program_id(0) == 0)
    def _():
        for k in range(-1, 16):
            for i, value in enumerate(weights_x(rank_ref, h_ref, k)):
                w_ref[i, k + 1] = jnp.broadcast_to(value, (8, 128))

    def weight(i, k):
        one = w_ref[i, k + 1]
        return jnp.concatenate([one, one], axis=1)

    def body(step, _):
        rows = pl.ds(pl.multiple_of(step * 8, 8), 8)
        loads = []
        x_even = x_ref[0, rows, :]
        carried = weight(3, -1) * (left_ref[rows, :] - weight(1, -1) * x_even)
        for j in range(16):
            x_odd = x_ref[2 * j + 1, rows, :]
            x_next = x_ref[2 * j + 2, rows, :] if j < 15 else right_ref[rows, :]
            detail = x_odd - weight(0, j) * x_even - weight(1, j) * x_next
            detail_ref[j, rows, :] = detail
            loads.append(weight(2, j) * detail + carried)
            carried = weight(3, j) * detail
            x_even = x_next
        for k in range(16):
            parts = [f_ref[k, j] * loads[j] for j in range(16)]
            while len(parts) > 1:
                parts = [parts[i] + parts[i + 1] for i in range(0, len(parts), 2)]
            v_ref[k, rows, :] = x_ref[2 * k, rows, :] + parts[0]
        return 0

    chunk = x_ref.shape[1]
    lax.fori_loop(0, chunk // 8, body, 0)
    values = v_ref[...].reshape(16 * chunk, 256)
    both = dot3(values, high_ref[...], low_ref[...])
    both = both.reshape(16, chunk, 256)
    dz_ref[...] = both[:, :, 0:128]
    cz_ref[...] = both[:, :, 128:256]
    lane = lax.broadcasted_iota(jnp.int32, (chunk, 128), 1)
    message = jnp.zeros((chunk, 128), F32)
    spread = lambda column: jnp.broadcast_to(column, (chunk, 128))
    for k in range(16):
        message = jnp.where(lane == k, spread(v_ref[k, :, 0:1]), message)
        message = jnp.where(lane == 16 + k, spread(dz_ref[k, :, 127:128]), message)
        tail = cz_ref[k, :, 127:128] - v_ref[k, :, 254:255]
        message = jnp.where(lane == 32 + k, spread(tail), message)
    column_ref[...] = message


def carry_kernel(g_ref, one_ref, two_ref, three_ref, high_ref, low_ref, row_ref, column_ref, plane_ref, out_ref):
    carry = two_ref[0:128, :] + two_ref[128:129, :] * three_ref[0:128, :]
    carry = one_ref[0:128, :] + one_ref[128:129, :] * carry
    plane = dot3(carry, high_ref[...], low_ref[...])
    plane_ref[...] = plane
    lane = lax.broadcasted_iota(jnp.int32, (1, 128), 1)
    gain = jnp.zeros((1, 128), F32)
    for k in range(48):
        gain = jnp.where(lane == k, g_ref[k % 16], gain)
    spread = lambda column: jnp.broadcast_to(column, (128, 128))
    wide = lax.broadcasted_iota(jnp.int32, (128, 128), 1)
    pieces = jnp.where(
        wide < 16,
        spread(carry[:, 0:1]),
        jnp.where(wide < 32, spread(plane[:, 127:128]), spread(plane[:, 255:256] - carry[:, 254:255])),
    )
    message = column_ref[...] + gain * pieces
    for i in range(3):
        message = jnp.where(wide == 48 + i, row_ref[4 + i : 5 + i, :], message)
    out_ref[...] = message


def last_kernel(
    rank_ref, g_ref, place_ref, dz_ref, cz_ref, plane_ref, all_ref, row_ref, detail_ref, out_ref
):
    rank = rank_ref[0]

    def clear(i, _):
        out_ref[pl.ds(pl.multiple_of(i * 16, 16), 16)] = jnp.zeros((16, 8, 128), F32)
        return 0

    lax.fori_loop(0, out_ref.shape[0] // 16, clear, 0)
    carry = jnp.zeros((128, 128), F32)
    for r in range(7):
        entering = carry * all_ref[r, 0:1, 50:51] + pltpu.roll(all_ref[r], 96, 1)
        entering = entering + all_ref[r, 0:1, 48:49] * all_ref[r + 1]
        if r > 0:
            entering = entering + all_ref[r, 0:1, 49:50] * pltpu.roll(all_ref[r - 1], 112, 1)
        carry = jnp.where(r < rank, entering, carry)
    right = jnp.where(rank < 7, all_ref[jnp.minimum(rank + 1, 7)], 0.0)
    left = pltpu.roll(all_ref[jnp.maximum(rank - 1, 0)], 112, 1)
    d_right, c_right, c_left, gain = (row_ref[i : i + 1, :] for i in range(4))
    spread = lambda value, k: jnp.broadcast_to(value[:, k : k + 1], (128, 128))
    top = lax.broadcasted_iota(jnp.int32, (8, 128), 0) < 4
    for k in range(16):
        g = g_ref[k]
        right_k = spread(right, k)
        detail = dz_ref[k] + g * plane_ref[:, 0:128] + right_k * d_right
        coarse = cz_ref[k] + g * plane_ref[:, 128:256] + right_k * c_right
        coarse = coarse + spread(left, k) * c_left + spread(carry, k) * gain
        detail_ref[k] = detail
        for i in range(16):
            c8, d8 = coarse[8 * i : 8 * i + 8], detail[8 * i : 8 * i + 8]
            block = 32 * k + 2 * i
            out_ref[place_ref[block]] = jnp.where(top, c8, pltpu.roll(d8, 4, 0))
            out_ref[place_ref[block + 1]] = jnp.where(top, pltpu.roll(c8, 4, 0), d8)


def shift(value, axis, by):
    count = lax.axis_size(axis)
    return lax.ppermute(value, axis, [(i, i + by) for i in range(count) if 0 <= i + by < count])


def local(
    nodal_field, spacing_x, spacing_z, operator_x, persist_x, operator_z, persist_z, receivers
):
    rank_x = lax.axis_index("gx").astype(jnp.int32).reshape(1)
    rank_z = lax.axis_index("gz").astype(jnp.int32).reshape(1)
    plane = jax.ShapeDtypeStruct((128, 256), F32)
    s, v = spec(SMEM), spec(VMEM)

    first, last = pl.pallas_call(
        edge_kernel,
        grid=(1,),
        in_specs=[
            s, s,
            pl.BlockSpec((2, 128, 256), lambda i: (0, 0, 0)),
            pl.BlockSpec((2, 128, 256), lambda i: (15, 0, 0)),
        ],
        out_specs=[pl.BlockSpec((128, 256), lambda i: (0, 0))] * 2,
        out_shape=[plane, plane],
        name="edge",
    )(rank_x, spacing_x, nodal_field, nodal_field)
    left = shift(last, "gx", 1)
    right = shift(first, "gx", -1)

    own = pl.pallas_call(
        tail_kernel,
        grid=(4,),
        in_specs=[s, s, s, pl.BlockSpec((32, 32, 256), lambda i: (0, i, 0))],
        out_specs=pl.BlockSpec((32, 256), lambda i: (i, 0)),
        out_shape=plane,
        cost_estimate=cost(64 * 32768, 4 << 20),
        name="tail",
    )(rank_x, spacing_x, operator_x, nodal_field)

    ended = pl.pallas_call(
        close_kernel,
        in_specs=[s, s, s, s, v, v, v],
        out_specs=v,
        out_shape=jax.ShapeDtypeStruct((136, 256), F32),
        name="close",
    )(rank_x, spacing_x, operator_x, persist_x, own, right, left)
    one, two, three = (shift(ended, "gx", by) for by in (1, 2, 3))

    near_space = lax.dynamic_slice_in_dim(spacing_z, rank_z[0] * 256, 256)
    high, low, rows = pl.pallas_call(
        table_kernel,
        in_specs=[s, s, v, v, v, v],
        out_specs=[v, v, v],
        out_shape=[
            jax.ShapeDtypeStruct((256, 256), BF16),
            jax.ShapeDtypeStruct((256, 256), BF16),
            jax.ShapeDtypeStruct((8, 128), F32),
        ],
        compiler_params=params(),
        cost_estimate=cost(6 * 256 * 256 * 128, 1 << 20),
        name="table",
    )(
        rank_z, spacing_z, near_space[0::2].reshape(1, 128), near_space[1::2].reshape(1, 128),
        operator_z, persist_z.reshape(1, 128),
    )

    chunk = 32
    whole = lambda shape: pl.BlockSpec(shape, lambda i: (0,) * len(shape))
    third = pl.BlockSpec((16, chunk, 128), lambda i: (0, i, 0))
    detail_x, dz, cz, columns = pl.pallas_call(
        main_kernel,
        grid=(128 // chunk,),
        in_specs=[
            s, s, s,
            pl.BlockSpec((32, chunk, 256), lambda i: (0, i, 0)),
            pl.BlockSpec((chunk, 256), lambda i: (i, 0)),
            pl.BlockSpec((chunk, 256), lambda i: (i, 0)),
            whole((256, 256)), whole((256, 256)),
        ],
        out_specs=[
            pl.BlockSpec((16, chunk, 256), lambda i: (0, i, 0)),
            third, third,
            pl.BlockSpec((chunk, 128), lambda i: (i, 0)),
        ],
        out_shape=[
            jax.ShapeDtypeStruct((16, 128, 256), F32),
            jax.ShapeDtypeStruct((16, 128, 128), F32),
            jax.ShapeDtypeStruct((16, 128, 128), F32),
            jax.ShapeDtypeStruct((128, 128), F32),
        ],
        scratch_shapes=[VMEM((4, 17, 8, 128), F32), VMEM((16, chunk, 256), F32)],
        compiler_params=params(),
        cost_estimate=cost(6 * 2048 * 256 * 256, 10 << 20),
        name="main",
    )(rank_x, spacing_x, operator_x, nodal_field, right, left, high, low)

    plane_pass, message = pl.pallas_call(
        carry_kernel,
        in_specs=[s, v, v, v, v, v, v, v],
        out_specs=[v, v],
        out_shape=[plane, jax.ShapeDtypeStruct((128, 128), F32)],
        compiler_params=params(),
        name="carry",
    )(persist_x, one, two, three, high, low, rows, columns)
    gathered = lax.all_gather(message, "gz")

    group = lax.axis_size("gy") * lax.axis_size("gz")
    capacity = 16
    targets = receivers[:, 0]
    positions = jnp.arange(512, dtype=jnp.int32)
    earlier = (targets[None, :] == targets[:, None]) & (positions[None, :] < positions[:, None])
    placed = targets * capacity + jnp.sum(earlier.astype(jnp.int32), axis=1)

    detail_z, outgoing = pl.pallas_call(
        last_kernel,
        in_specs=[s, s, s, v, v, v, v, v],
        out_specs=[v, v],
        out_shape=[
            jax.ShapeDtypeStruct((16, 128, 128), F32),
            jax.ShapeDtypeStruct((group * capacity, 8, 128), F32),
        ],
        compiler_params=params(),
        name="last",
    )(rank_z, persist_x, placed, dz, cz, plane_pass, gathered, rows)
    incoming = lax.all_to_all(
        outgoing.reshape(group, capacity, 8, 128), ("gy", "gz"), split_axis=0, concat_axis=0, tiled=True
    )
    received = incoming.reshape(1, group, capacity, 2, LINES, 128)
    return (detail_x, detail_z, received)


def solution(mesh):
    return jax.shard_map(
        local,
        mesh=mesh,
        in_specs=(
            P("gx", "gy", "gz"),
            P(),
            P(),
            P("gx", None),
            P("gx"),
            P("gz", None),
            P("gz"),
            P(("gx", "gy", "gz"), None),
        ),
        out_specs=(
            P("gx", "gy", "gz"),
            P("gx", "gy", "gz"),
            P(("gx", "gy", "gz"), None, None, None, None, None),
        ),
        check_vma=False,
    )
```

time: 248 us -> 164 us (0.66)
  waiting for transfers between devices: 94.4 us -> 0.01 us
  blocking collectives: 47.5 us -> 121 us
  local copies, waits for them, and re-layouts: 49.3 us -> 5.67 us
  Pallas kernels: 0 us -> 21.7 us
  other arithmetic: 16.5 us -> 0.25 us
  matrix products: 9.33 us -> 0 us
  starting transfers between devices: 22.7 us -> 13.7 us
  between operations: 7.52 us -> 0.84 us
    all_to_all x0 -> x1, blocking collectives: none -> 108 us  [local(): lax.all_to_all(outgoing.reshape(group, capacity, 8, 128), ('gy', 'gz'), s...]
    all_to_all x1 -> x0, waiting for transfers between devices: 94.3 us -> none  [local(): lax.all_to_all(outgoing, ('gy', 'gz'), split_axis=0, concat_axis=0, tiled...]
    unnamed x2 -> x0, blocking collectives: 21.8 us -> none
    pallas_call x0 -> x7, Pallas kernels: none -> 21.7 us  [the longest x1 7.63 us: local(): pl.pallas_call(main_kernel, grid=(128 // chunk,), in_specs=[s, s, s, pl.B...]
    all_to_all x1 -> x0, starting transfers between devices: 13 us -> none  [local(): lax.all_to_all(outgoing, ('gy', 'gz'), split_axis=0, concat_axis=0, tiled...]
    slice x18 -> x2, local copies, waits for them, and re-layouts: 13 us -> 0.45 us  [the longest x1 0.23 us: local(): near_space[0::2].reshape(1, 128)]
    all_gather x2 -> x1, blocking collectives: 25.7 us -> 13.3 us  [local(): gathered = lax.all_gather(message, 'gz')]
    dynamic_slice x24 -> x1, local copies, waits for them, and re-layouts: 9.48 us -> 0.08 us  [local(): near_space = lax.dynamic_slice_in_dim(spacing_z, rank_z[0] * 256, 256)]
  transfers between devices with their start and end apart: 5 -> 5, of which waited for: 2 -> 0; matrix products, arithmetic and copies ran while one was open for 9% -> 0% of each run, Pallas kernels for 0% -> 8%
where the time goes in v1:
time: 164 us; the launch traced here: 163 us
  blocking collectives  121 us (74%)
  Pallas kernels  21.7 us (13%)
  starting transfers between devices  13.7 us (8%)
  local copies, waits for them, and re-layouts  5.67 us (3%)
    all_to_all x1, blocking collectives, local(): lax.all_to_all(outgoing.reshape(group, capacity, 8, 128), ('gy', 'gz'), s...  108 us
    ppermute x5, starting transfers between devices, shift(): lax.ppermute(value, axis, [(i, i + by) for i in range(count) if 0 <= i +...  13.7 us
    all_gather x1, blocking collectives, local(): gathered = lax.all_gather(message, 'gz')  13.3 us
    pallas_call x1, Pallas kernels, local(): pl.pallas_call(main_kernel, grid=(128 // chunk,), in_specs=[s, s, s, pl.B...  7.63 us
    unnamed x23, local copies, waits for them, and re-layouts  5.15 us
    pallas_call x1, Pallas kernels, local(): pl.pallas_call(last_kernel, in_specs=[s, s, s, v, v, v, v, v], out_specs=...  4.56 us
    pallas_call x1, Pallas kernels, local(): pl.pallas_call(tail_kernel, grid=(4,), in_specs=[s, s, s, pl.BlockSpec((3...  4.06 us
  transfers between devices with their start and end apart: 5, of which 0 were waited for; matrix products, arithmetic and copies ran while one was open for 0% of the time, Pallas kernels for 8%

profile of v1, /device:TPU:8, one launch (start us, length us, event | category | flops | bytes accessed | tf_op | source)
XLA Modules:
  0.0 163.4 jit_solution(8749758561078148429)
XLA Ops:
  0.6 1.8 %edge.1 = (f32[128,256]{1,0:T(8,128)}, f32[128,256]{1,0:T(8,128)}) custom-call(s32[1]{0:T(128)} %bitcast.rank_ref, f32[128]{0:T(128)} %h_ref.9, f32[32,128,256]{2,1,0:T(8,128)} %x_ref.3, f32[32,128,256]{2,1,0:T(8,128)} %x_ref.3), custom_call_target="tpu_custom_call" | custom-call | tf_op jit(solution)/shard_map/edge/pallas_call | solution.py:255
  2.4 0.0 copy-start.9
  2.4 0.0 copy-start.4
  2.4 0.0 copy-start.5
  2.4 1.4 collective-permute-start
  3.9 0.0 copy-start.6
  3.9 4.6 %collective-permute-start.1 = (f32[128,256]{1,0:T(8,128)}, f32[128,256]{1,0:T(8,128)S(1)}, u32[]{:S(2)}, u32[]{:S(2)}) collective-permute-start(f32[128,256]{1,0:T(8,128)} %get-tuple-element.17), channel_id=1, source_target_pairs={{0,64},{64,128},{128,192},{1,65},{65,129},{129,193},{2,66},{66,130... | collective-permute-start | bytes 393224 | tf_op jit(solution)/shard_map/ppermute | solution.py:244
  8.4 4.1 %tail.1.own_ref = f32[128,256]{1,0:T(8,128)} custom-call(s32[1]{0:T(128)} %bitcast.rank_ref, f32[128]{0:T(128)} %h_ref.9, f32[16,16]{1,0:T(8,128)} %f_ref.7, f32[32,128,256]{2,1,0:T(8,128)} %x_ref.3), custom_call_target="tpu_custom_call" | custom-call | flops 2097152 | bytes 4194304 | tf_op jit(solution)/shard_map/tail/pallas_call | solution.py:270
  12.5 0.2 convert_reduce_fusion
  12.8 0.0 copy-start
  12.8 0.0 collective-permute-done.1.left_ref
  12.8 0.6 copy-done
  13.4 0.7 copy-done.2
  14.1 1.7 %close.1 = f32[136,256]{1,0:T(8,128)} custom-call(s32[1]{0:T(128)} %bitcast.rank_ref, f32[128]{0:T(128)} %h_ref.9, f32[16,16]{1,0:T(8,128)} %f_ref.7, f32[16]{0:T(128)} %g_ref.5, f32[128,256]{1,0:T(8,128)} %tail.1.own_ref, f32[128,256]{1,0:T(8,128)} %copy-done, f32[128,256]{1,0:T(8,128)} %copy-done.2), custom_call_target="tpu_custom_call" | custom-call | tf_op jit(solution)/shard_map/close/pallas_call | solution.py:280
  15.8 3.6 %collective-permute-start.4 = (f32[136,256]{1,0:T(8,128)}, f32[136,256]{1,0:T(8,128)S(1)}, u32[]{:S(2)}, u32[]{:S(2)}) collective-permute-start(f32[136,256]{1,0:T(8,128)} %close.1), channel_id=1, source_target_pairs={{0,192},{1,193},{2,194},{3,195},{4,196},{5,197},{6,198},{7,199},{8... | collective-permute-start | bytes 417800 | tf_op jit(solution)/shard_map/ppermute | solution.py:244
  19.4 2.0 %collective-permute-start.3 = (f32[136,256]{1,0:T(8,128)}, f32[136,256]{1,0:T(8,128)S(1)}, u32[]{:S(2)}, u32[]{:S(2)}) collective-permute-start(f32[136,256]{1,0:T(8,128)} %close.1), channel_id=1, source_target_pairs={{0,128},{64,192},{1,129},{65,193},{2,130},{66,194},{3,131},{67,195... | collective-permute-start | bytes 417800 | tf_op jit(solution)/shard_map/ppermute | solution.py:244
  21.4 2.1 %collective-permute-start.2 = (f32[136,256]{1,0:T(8,128)}, f32[136,256]{1,0:T(8,128)S(1)}, u32[]{:S(2)}, u32[]{:S(2)}) collective-permute-start(f32[136,256]{1,0:T(8,128)} %close.1), channel_id=1, source_target_pairs={{0,64},{64,128},{128,192},{1,65},{65,129},{129,193},{2,66},{66,130... | collective-permute-start | bytes 417800 | tf_op jit(solution)/shard_map/ppermute | solution.py:244
  23.6 0.1 dynamic_slice.3
  23.6 0.2 slice.7
  23.9 0.2 slice.6
  24.1 1.1 table.1
  25.2 0.0 copy-start.1
  25.3 0.9 copy-done.1
  26.1 0.9 copy-done.3
  27.1 7.6 %main.1 = (f32[16,128,256]{2,1,0:T(8,128)}, f32[16,128,128]{2,1,0:T(8,128)S(1)}, f32[16,128,128]{2,1,0:T(8,128)S(1)}, f32[128,128]{1,0:T(8,128)S(1)}) custom-call(s32[1]{0:T(128)} %bitcast.rank_ref, f32[128]{0:T(128)S(1)} %copy-done.5, f32[16,16]{1,0:T(8,128)S(1)} %copy-done.4, f32[32,128,256]{2,1,0:T(8,128)} %x_ref.3, f32[128,256]{1,0:T(8,128)S(1)} %copy-done.1, ...), custom_call_target="tpu_custom_call" | custom-call | flops 805306368 | bytes 10485760 | tf_op jit(solution)/shard_map/main/pallas_call | solution.py:310
  34.7 0.0 collective-permute-done.4.three_ref
  34.7 0.0 collective-permute-done.3.two_ref
  34.7 0.9 carry.1
  35.6 13.3 %all-gather = f32[1024,128]{1,0:T(8,128)S(1)} all-gather(f32[128,128]{1,0:T(8,128)S(1)} %get-tuple-element.26), channel_id=2, replica_groups=mesh['gx'=4,'gy'=8,'gz'=8] {'gz'}, dimensions={0}, use_global_device_ids=true | all-gather | bytes 589824 | tf_op jit(solution)/shard_map/all_gather | solution.py:345
  48.9 4.6 %last.1 = (f32[16,128,128]{2,1,0:T(8,128)}, f32[1024,8,128]{2,1,0:T(8,128)}) custom-call(s32[1]{0:T(128)} %bitcast.1.rank_ref, f32[16]{0:T(128)S(1)} %copy-done.6, s32[512]{0:T(512)S(1)} %multiply_add_fusion.place_ref, f32[16,128,128]{2,1,0:T(8,128)S(1)} %get-tuple-element.21.dz_ref, f32[16,128,128]{2,1,0:T(8,128)S(1)} %get-tuple-element.22.cz_ref, ...), custom_call_target="tpu_custom_call" | custom-call | tf_op jit(solution)/shard_map/last/pallas_call | solution.py:354
  53.5 107.9 %all_to_all.5 = f32[64,16,8,128]{3,2,1,0:T(8,128)S(1)} all-to-all(f32[64,16,8,128]{3,2,1,0:T(8,128)} %bitcast.14), channel_id=1, replica_groups=mesh['gx'=4,'gy'=8,'gz'=8] {'gy','gz'}, dimensions={0} | all-to-all | bytes 8388608 | tf_op jit(solution)/shard_map/all_to_all | solution.py:365
  161.4 2.0 %copy.12 = f32[1,64,16,2,4,128]{5,4,3,2,1,0:T(4,128)} copy(f32[1,64,16,2,4,128]{5,4,3,2,1,0:T(4,128)S(1)} %bitcast.13) | data formatting | bytes 8388608
  (15 shorter events, 0.0 us)
Async XLA Ops:
  2.4 10.1 %copy-start.10 = (s32[512,1]{0,1:T(1,128)S(1)}, s32[512,1]{0,1:T(1,128)}, u32[]{:S(2)}) copy-start(s32[512,1]{0,1:T(1,128)} %param.15) | copy-start | bytes 6148
  2.4 21.2 %copy-start.7 = (f32[2048]{0:T(1024)S(1)}, f32[2048]{0:T(1024)}, u32[]{:S(2)}) copy-start(f32[2048]{0:T(1024)} %h_ref.6) | copy-start | bytes 24580
  2.4 21.7 %copy-start.8 = (f32[128,128]{1,0:T(8,128)S(1)}, f32[128,128]{1,0:T(8,128)}, u32[]{:S(2)}) copy-start(f32[128,128]{1,0:T(8,128)} %f_ref.4) | copy-start | bytes 196612
  2.4 21.7 %copy-start.9 = (f32[128]{0:T(128)S(1)}, f32[128]{0:T(128)}, u32[]{:S(2)}) copy-start(f32[128]{0:T(128)} %param.14) | copy-start | bytes 1540
  2.4 22.8 %copy-start.4 = (f32[16,16]{1,0:T(8,128)S(1)}, f32[16,16]{1,0:T(8,128)}, u32[]{:S(2)}) copy-start(f32[16,16]{1,0:T(8,128)} %f_ref.7) | copy-start | bytes 3076
  2.4 22.8 %copy-start.5 = (f32[128]{0:T(128)S(1)}, f32[128]{0:T(128)}, u32[]{:S(2)}) copy-start(f32[128]{0:T(128)} %h_ref.9) | copy-start | bytes 1540
  2.4 10.3 %collective-permute-start = (f32[128,256]{1,0:T(8,128)}, f32[128,256]{1,0:T(8,128)S(1)}, u32[]{:S(2)}, u32[]{:S(2)}) collective-permute-start(f32[128,256]{1,0:T(8,128)} %get-tuple-element.16), channel_id=1, source_target_pairs={{64,0},{128,64},{192,128},{65,1},{129,65},{193,129},{66,2},{130,66... | collective-permute-start | bytes 393224 | tf_op jit(solution)/shard_map/ppermute | solution.py:244
  3.9 30.8 %copy-start.6 = (f32[16]{0:T(128)S(1)}, f32[16]{0:T(128)}, u32[]{:S(2)}) copy-start(f32[16]{0:T(128)} %g_ref.5) | copy-start | bytes 196
  3.9 8.9 %collective-permute-start.1 = (f32[128,256]{1,0:T(8,128)}, f32[128,256]{1,0:T(8,128)S(1)}, u32[]{:S(2)}, u32[]{:S(2)}) collective-permute-start(f32[128,256]{1,0:T(8,128)} %get-tuple-element.17), channel_id=1, source_target_pairs={{0,64},{64,128},{128,192},{1,65},{65,129},{129,193},{2,66},{66,130... | collective-permute-start | bytes 393224 | tf_op jit(solution)/shard_map/ppermute | solution.py:244
  12.8 0.7 copy-start
  13.4 0.7 copy-start.2
  15.8 18.9 %collective-permute-start.4 = (f32[136,256]{1,0:T(8,128)}, f32[136,256]{1,0:T(8,128)S(1)}, u32[]{:S(2)}, u32[]{:S(2)}) collective-permute-start(f32[136,256]{1,0:T(8,128)} %close.1), channel_id=1, source_target_pairs={{0,192},{1,193},{2,194},{3,195},{4,196},{5,197},{6,198},{7,199},{8... | collective-permute-start | bytes 417800 | tf_op jit(solution)/shard_map/ppermute | solution.py:244
  19.4 15.2 %collective-permute-start.3 = (f32[136,256]{1,0:T(8,128)}, f32[136,256]{1,0:T(8,128)S(1)}, u32[]{:S(2)}, u32[]{:S(2)}) collective-permute-start(f32[136,256]{1,0:T(8,128)} %close.1), channel_id=1, source_target_pairs={{0,128},{64,192},{1,129},{65,193},{2,130},{66,194},{3,131},{67,195... | collective-permute-start | bytes 417800 | tf_op jit(solution)/shard_map/ppermute | solution.py:244
  21.4 13.3 %collective-permute-start.2 = (f32[136,256]{1,0:T(8,128)}, f32[136,256]{1,0:T(8,128)S(1)}, u32[]{:S(2)}, u32[]{:S(2)}) collective-permute-start(f32[136,256]{1,0:T(8,128)} %close.1), channel_id=1, source_target_pairs={{0,64},{64,128},{128,192},{1,65},{65,129},{129,193},{2,66},{66,130... | collective-permute-start | bytes 417800 | tf_op jit(solution)/shard_map/ppermute | solution.py:244
  25.2 0.9 copy-start.1
  26.1 0.9 copy-start.3

commit v2 on v1

v2 whole, which is shorter than its diff:
```python
import jax
import jax.numpy as jnp
from jax import lax
from jax.experimental import pallas as pl
from jax.experimental.pallas import tpu as pltpu
from jax.sharding import PartitionSpec as P

LINES = 4
F32 = jnp.float32
BF16 = jnp.bfloat16
SMEM = pltpu.SMEM
VMEM = pltpu.VMEM


def spec(space):
    return pl.BlockSpec(memory_space=space)


def cost(flops, moved):
    return pl.CostEstimate(flops=flops, bytes_accessed=moved, transcendentals=0)


def params(mib=16):
    return pltpu.CompilerParams(vmem_limit_bytes=mib << 20)


def weights_x(rank_ref, h_ref):
    own = pltpu.roll(jnp.broadcast_to(h_ref[...], (8, 128)), 128 - 32 * rank_ref[0], 1)
    after = pltpu.roll(own, 127, 1)
    total = own + after
    return after / total, own / total, 0.5 * own, 0.5 * after


def head_kernel(rank_ref, f_ref, h_ref, x_ref, first_ref, last_ref, out_ref):
    rows_of = weights_x(rank_ref, h_ref)
    weight = lambda i, k: rows_of[i][0:1, (2 * k) % 128 : (2 * k) % 128 + 1]
    far_before = jnp.where(rank_ref[0] > 0, weight(3, -1), 0.0)
    before = -f_ref[15, 0] * far_before * weight(1, -1)
    total = None
    for j in range(16):
        v = f_ref[15, j] * weight(2, j)
        if j < 15:
            v = v + f_ref[15, j + 1] * weight(3, j)
        term = (before - v * weight(0, j)) * x_ref[2 * j] + v * x_ref[2 * j + 1]
        total = term if total is None else total + term
        before = -v * weight(1, j)
    out_ref[...] = total
    first_ref[...] = x_ref[0]
    last_ref[...] = x_ref[31] - weight(0, 15) * x_ref[30]


def close_kernel(g_ref, row_ref, own_ref, right_ref, left_ref, out_ref):
    total = own_ref[...] + row_ref[15:16, 0:1] * right_ref[...] + row_ref[31:32, 0:1] * left_ref[...]
    out_ref[0:128, :] = total
    out_ref[128:136, :] = jnp.full((8, 256), g_ref[15], F32)


def split(value):
    high = value.astype(BF16)
    return high, (value - high.astype(F32)).astype(BF16)


def dot3(value, high, low):
    v_high, v_low = split(value)
    one = lambda a, b: jnp.dot(a, b, preferred_element_type=F32)
    return one(v_high, high) + (one(v_low, high) + one(v_high, low))


def dot_nt(a, b):
    return lax.dot_general(
        a, b, (((1,), (1,)), ((), ())), precision=lax.Precision.HIGHEST, preferred_element_type=F32
    )


def pass_matrix(even, odd, far_before, b_before, factor, nodes):
    total = even + odd
    a, b = odd / total, even / total
    near, far = 0.5 * even, 0.5 * odd
    z = lax.broadcasted_iota(jnp.int32, (nodes, 128), 0)
    k = lax.broadcasted_iota(jnp.int32, (nodes, 128), 1)
    chosen = jnp.where(z == 2 * k, 1.0, 0.0)
    detail = jnp.where(z == 2 * k + 1, 1.0, 0.0) - chosen * a - jnp.where(z == 2 * k + 2, b, 0.0)
    shifted = jnp.where(k == 0, 0.0, pltpu.roll(detail * far, 1, 1))
    load = detail * near + shifted
    load = load - jnp.where((z == 0) & (k == 0), far_before * b_before, 0.0)
    half = nodes // 2
    return detail, chosen[:, 0:half] + dot_nt(load[:, 0:half], factor), near, b


def table_kernel(
    rank_ref, rank_x_ref, h_ref, even_ref, odd_ref, f_ref, g_ref, hx_ref, fx_ref,
    high_ref, low_ref, row_ref, x_high_ref, x_low_ref, x_row_ref,
):
    at = jnp.maximum(rank_ref[0] * 256 - 2, 0)
    one = lambda value: jnp.full((1, 1), value, F32)
    h_even, h_odd = one(h_ref[at]), one(h_ref[at + 1])
    far_before = jnp.where(rank_ref[0] > 0, 0.5 * h_odd, 0.0)
    detail, coarse, near, b = pass_matrix(
        even_ref[...], odd_ref[...], far_before, h_even / (h_even + h_odd), f_ref[...], 256
    )
    high, low = split(detail)
    high_ref[:, 0:128], low_ref[:, 0:128] = high, low
    high, low = split(coarse)
    high_ref[:, 128:256], low_ref[:, 128:256] = high, low
    row = lax.broadcasted_iota(jnp.int32, (8, 128), 0)
    lane = lax.broadcasted_iota(jnp.int32, (8, 128), 1)
    pick = jnp.where(((row == 1) & (lane == 127)) | ((row == 2) & (lane == 0)), 1.0, 0.0)
    columns = dot_nt(pick, f_ref[...])
    last = lane[0:1] == 127
    from_right = columns[1:2] * (-near[:, 127:128] * b[:, 127:128])
    from_left = columns[2:3] * far_before
    gain = g_ref[...]
    row_ref[0:1] = jnp.where(last, -b, 0.0)
    row_ref[1:2] = from_right
    row_ref[2:3] = from_left
    row_ref[3:4] = gain
    row_ref[4:5] = jnp.broadcast_to(from_right[:, 127:128], (1, 128))
    row_ref[5:6] = jnp.broadcast_to(from_left[:, 127:128], (1, 128))
    row_ref[6:7] = jnp.broadcast_to(gain[:, 127:128], (1, 128))
    row_ref[7:8] = jnp.zeros((1, 128), F32)

    base = rank_x_ref[0] * 32
    node = lax.broadcasted_iota(jnp.int32, (128, 128), 0)
    place = lax.broadcasted_iota(jnp.int32, (128, 128), 1)
    index = jnp.where(place == 127, jnp.maximum(base - 2, 0), base + 2 * jnp.minimum(place, 15))
    h = jnp.broadcast_to(hx_ref[...], (8, 128))
    take = lambda where: jnp.dot(
        h, jnp.where(node == where, 1.0, 0.0), precision=lax.Precision.HIGHEST, preferred_element_type=F32
    )[0:1]
    even, odd = take(index), take(index + 1)
    far_before = jnp.where(rank_x_ref[0] > 0, 0.5 * odd[:, 127:128], 0.0)
    b_before = even[:, 127:128] / (even[:, 127:128] + odd[:, 127:128])
    factor = fx_ref[...]
    _, coarse, near, b = pass_matrix(even, odd, far_before, b_before, factor, 32)
    one_of = lambda n, m: jnp.where(
        lax.broadcasted_iota(jnp.int32, (n, m), 0) // 8 == lax.broadcasted_iota(jnp.int32, (n, m), 1), 1.0, 0.0
    )
    tall = jnp.dot(
        one_of(256, 32), coarse, precision=lax.Precision.HIGHEST, preferred_element_type=F32
    )
    both = dot_nt(one_of(128, 16), tall)
    same = (
        lax.broadcasted_iota(jnp.int32, (128, 256), 0) % 8
        == lax.broadcasted_iota(jnp.int32, (128, 256), 1) % 8
    )
    high, low = split(jnp.where(same, both, 0.0))
    x_high_ref[...], x_low_ref[...] = high, low
    x_row_ref[0:16, :] = jnp.broadcast_to(factor[:, 15:16] * (-near[:, 15:16] * b[:, 15:16]), (16, 128))
    x_row_ref[16:32, :] = jnp.broadcast_to(factor[:, 0:1] * far_before, (16, 128))


def dot3_left(high, low, value):
    v_high, v_low = split(value)
    one = lambda a, b: jnp.dot(a, b, preferred_element_type=F32)
    return one(high, v_high) + (one(high, v_low) + one(low, v_high))


def main_kernel(
    x_row_ref, x_ref, right_ref, left_ref, x_high_ref, x_low_ref, high_ref, low_ref,
    dz_ref, cz_ref, column_ref, v_ref,
):
    chunk = x_ref.shape[1]
    for step in range(chunk // 8):
        rows = slice(step * 8, step * 8 + 8)
        nodes = x_ref[:, rows, :].reshape(256, 256)
        coarse = dot3_left(x_high_ref[...], x_low_ref[...], nodes)
        for k in range(16):
            v_ref[k, rows, :] = (
                coarse[8 * k : 8 * k + 8]
                + x_row_ref[k : k + 1, 0:1] * right_ref[rows, :]
                + x_row_ref[16 + k : 17 + k, 0:1] * left_ref[rows, :]
            )
    values = v_ref[...].reshape(16 * chunk, 256)
    both = dot3(values, high_ref[...], low_ref[...])
    both = both.reshape(16, chunk, 256)
    dz_ref[...] = both[:, :, 0:128]
    cz_ref[...] = both[:, :, 128:256]
    lane = lax.broadcasted_iota(jnp.int32, (chunk, 128), 1)
    message = jnp.zeros((chunk, 128), F32)
    spread = lambda column: jnp.broadcast_to(column, (chunk, 128))
    for k in range(16):
        message = jnp.where(lane == k, spread(v_ref[k, :, 0:1]), message)
        message = jnp.where(lane == 16 + k, spread(dz_ref[k, :, 127:128]), message)
        tail = cz_ref[k, :, 127:128] - v_ref[k, :, 254:255]
        message = jnp.where(lane == 32 + k, spread(tail), message)
    column_ref[...] = message


def output_kernel(
    rank_ref, rank_x_ref, g_ref, h_ref, x_ref, right_ref, dz_ref, plane_ref, all_ref, row_ref,
    detail_x_ref, detail_z_ref,
):
    rows_of = weights_x(rank_x_ref, h_ref)
    weight = lambda i, k: rows_of[i][0:1, 2 * k : 2 * k + 1]
    for j in range(16):
        after = x_ref[2 * j + 2] if j < 15 else right_ref[...]
        detail_x_ref[j] = x_ref[2 * j + 1] - weight(0, j) * x_ref[2 * j] - weight(1, j) * after
    rank = rank_ref[0]
    chunk = x_ref.shape[1]
    rows = pl.ds(pl.multiple_of(pl.program_id(0) * chunk, chunk), chunk)
    edge = jnp.where(rank < 7, all_ref[jnp.minimum(rank + 1, 7), rows, :], 0.0)
    for k in range(16):
        spread = jnp.broadcast_to(edge[:, k : k + 1], (chunk, 128))
        detail_z_ref[k] = dz_ref[k] + g_ref[k] * plane_ref[:, 0:128] + spread * row_ref[0:1, :]


def carry_kernel(g_ref, one_ref, two_ref, three_ref, high_ref, low_ref, row_ref, column_ref, plane_ref, out_ref):
    carry = two_ref[0:128, :] + two_ref[128:129, :] * three_ref[0:128, :]
    carry = one_ref[0:128, :] + one_ref[128:129, :] * carry
    plane = dot3(carry, high_ref[...], low_ref[...])
    plane_ref[...] = plane
    lane = lax.broadcasted_iota(jnp.int32, (1, 128), 1)
    gain = jnp.zeros((1, 128), F32)
    for k in range(48):
        gain = jnp.where(lane == k, g_ref[k % 16], gain)
    spread = lambda column: jnp.broadcast_to(column, (128, 128))
    wide = lax.broadcasted_iota(jnp.int32, (128, 128), 1)
    pieces = jnp.where(
        wide < 16,
        spread(carry[:, 0:1]),
        jnp.where(wide < 32, spread(plane[:, 127:128]), spread(plane[:, 255:256] - carry[:, 254:255])),
    )
    message = column_ref[...] + gain * pieces
    for i in range(3):
        message = jnp.where(wide == 48 + i, row_ref[4 + i : 5 + i, :], message)
    out_ref[...] = message


def last_kernel(
    rank_ref, g_ref, place_ref, dz_ref, cz_ref, plane_ref, all_ref, row_ref, out_ref
):
    rank = rank_ref[0]

    def clear(i, _):
        out_ref[pl.ds(pl.multiple_of(i * 16, 16), 16)] = jnp.zeros((16, 8, 128), F32)
        return 0

    lax.fori_loop(0, out_ref.shape[0] // 16, clear, 0)
    carry = jnp.zeros((128, 128), F32)
    for r in range(7):
        entering = carry * all_ref[r, 0:1, 50:51] + pltpu.roll(all_ref[r], 96, 1)
        entering = entering + all_ref[r, 0:1, 48:49] * all_ref[r + 1]
        if r > 0:
            entering = entering + all_ref[r, 0:1, 49:50] * pltpu.roll(all_ref[r - 1], 112, 1)
        carry = jnp.where(r < rank, entering, carry)
    right = jnp.where(rank < 7, all_ref[jnp.minimum(rank + 1, 7)], 0.0)
    left = pltpu.roll(all_ref[jnp.maximum(rank - 1, 0)], 112, 1)
    d_right, c_right, c_left, gain = (row_ref[i : i + 1, :] for i in range(4))
    spread = lambda value, k: jnp.broadcast_to(value[:, k : k + 1], (128, 128))
    top = lax.broadcasted_iota(jnp.int32, (8, 128), 0) < 4
    for k in range(16):
        g = g_ref[k]
        right_k = spread(right, k)
        detail = dz_ref[k] + g * plane_ref[:, 0:128] + right_k * d_right
        coarse = cz_ref[k] + g * plane_ref[:, 128:256] + right_k * c_right
        coarse = coarse + spread(left, k) * c_left + spread(carry, k) * gain
        for i in range(16):
            c8, d8 = coarse[8 * i : 8 * i + 8], detail[8 * i : 8 * i + 8]
            block = 32 * k + 2 * i
            out_ref[place_ref[block]] = jnp.where(top, c8, pltpu.roll(d8, 4, 0))
            out_ref[place_ref[block + 1]] = jnp.where(top, pltpu.roll(c8, 4, 0), d8)


def shift(value, axis, by):
    count = lax.axis_size(axis)
    return lax.ppermute(value, axis, [(i, i + by) for i in range(count) if 0 <= i + by < count])


def local(
    nodal_field, spacing_x, spacing_z, operator_x, persist_x, operator_z, persist_z, receivers
):
    rank_x = lax.axis_index("gx").astype(jnp.int32).reshape(1)
    rank_z = lax.axis_index("gz").astype(jnp.int32).reshape(1)
    plane = jax.ShapeDtypeStruct((128, 256), F32)
    s, v = spec(SMEM), spec(VMEM)

    chunk = 32
    whole = lambda shape: pl.BlockSpec(shape, lambda i: (0,) * len(shape))
    nodes = pl.BlockSpec((32, chunk, 256), lambda i: (0, i, 0))
    thin = pl.BlockSpec((chunk, 256), lambda i: (i, 0))
    third = pl.BlockSpec((16, chunk, 128), lambda i: (0, i, 0))
    grid = (128 // chunk,)
    space_x = spacing_x.reshape(1, 128)

    first, last, own = pl.pallas_call(
        head_kernel,
        grid=grid,
        in_specs=[s, s, whole((1, 128)), nodes],
        out_specs=[thin, thin, thin],
        out_shape=[plane, plane, plane],
        cost_estimate=cost(64 * 32768, 4 << 20),
        name="head",
    )(rank_x, operator_x, space_x, nodal_field)
    left = shift(last, "gx", 1)
    right = shift(first, "gx", -1)

    near_space = lax.dynamic_slice_in_dim(spacing_z, rank_z[0] * 256, 256)
    square = jax.ShapeDtypeStruct((256, 256), BF16)
    oblong = jax.ShapeDtypeStruct((128, 256), BF16)
    high, low, rows, x_high, x_low, x_rows = pl.pallas_call(
        table_kernel,
        in_specs=[s, s, s, v, v, v, v, v, v],
        out_specs=[v] * 6,
        out_shape=[
            square, square, jax.ShapeDtypeStruct((8, 128), F32),
            oblong, oblong, jax.ShapeDtypeStruct((32, 128), F32),
        ],
        compiler_params=params(),
        cost_estimate=cost(12 * 256 * 256 * 128, 1 << 20),
        name="table",
    )(
        rank_z, rank_x, spacing_z, near_space[0::2].reshape(1, 128), near_space[1::2].reshape(1, 128),
        operator_z, persist_z.reshape(1, 128), space_x, operator_x,
    )

    ended = pl.pallas_call(
        close_kernel,
        in_specs=[s, v, v, v, v],
        out_specs=v,
        out_shape=jax.ShapeDtypeStruct((136, 256), F32),
        name="close",
    )(persist_x, x_rows, own, right, left)
    one, two, three = (shift(ended, "gx", by) for by in (1, 2, 3))

    dz, cz, columns = pl.pallas_call(
        main_kernel,
        grid=grid,
        in_specs=[
            whole((32, 128)), nodes, thin, thin,
            whole((128, 256)), whole((128, 256)), whole((256, 256)), whole((256, 256)),
        ],
        out_specs=[third, third, pl.BlockSpec((chunk, 128), lambda i: (i, 0))],
        out_shape=[
            jax.ShapeDtypeStruct((16, 128, 128), F32),
            jax.ShapeDtypeStruct((16, 128, 128), F32),
            jax.ShapeDtypeStruct((128, 128), F32),
        ],
        scratch_shapes=[VMEM((16, chunk, 256), F32)],
        compiler_params=params(),
        cost_estimate=cost(6 * 2048 * 256 * 256, 10 << 20),
        name="main",
    )(x_rows, nodal_field, right, left, x_high, x_low, high, low)

    plane_pass, message = pl.pallas_call(
        carry_kernel,
        in_specs=[s, v, v, v, v, v, v, v],
        out_specs=[v, v],
        out_shape=[plane, jax.ShapeDtypeStruct((128, 128), F32)],
        compiler_params=params(),
        name="carry",
    )(persist_x, one, two, three, high, low, rows, columns)
    gathered = lax.all_gather(message, "gz")

    group = lax.axis_size("gy") * lax.axis_size("gz")
    capacity = 16
    targets = receivers[:, 0]
    positions = jnp.arange(512, dtype=jnp.int32)
    earlier = (targets[None, :] == targets[:, None]) & (positions[None, :] < positions[:, None])
    placed = targets * capacity + jnp.sum(earlier.astype(jnp.int32), axis=1)

    outgoing = pl.pallas_call(
        last_kernel,
        in_specs=[s, s, s, v, v, v, v, v],
        out_specs=v,
        out_shape=jax.ShapeDtypeStruct((group * capacity, 8, 128), F32),
        compiler_params=params(),
        name="last",
    )(rank_z, persist_x, placed, dz, cz, plane_pass, gathered, rows)
    incoming = lax.all_to_all(
        outgoing.reshape(group, capacity, 8, 128), ("gy", "gz"), split_axis=0, concat_axis=0, tiled=True
    )
    detail_x, detail_z = pl.pallas_call(
        output_kernel,
        grid=grid,
        in_specs=[
            s, s, s, whole((1, 128)), nodes, thin, third, thin, whole((8, 128, 128)), whole((8, 128)),
        ],
        out_specs=[pl.BlockSpec((16, chunk, 256), lambda i: (0, i, 0)), third],
        out_shape=[
            jax.ShapeDtypeStruct((16, 128, 256), F32),
            jax.ShapeDtypeStruct((16, 128, 128), F32),
        ],
        compiler_params=params(),
        cost_estimate=cost(1 << 20, 8 << 20),
        name="output",
    )(rank_z, rank_x, persist_x, space_x, nodal_field, right, dz, plane_pass, gathered, rows)
    received = incoming.reshape(1, group, capacity, 2, LINES, 128)
    return (detail_x, detail_z, received)


def solution(mesh):
    return jax.shard_map(
        local,
        mesh=mesh,
        in_specs=(
            P("gx", "gy", "gz"),
            P(),
            P(),
            P("gx", None),
            P("gx"),
            P("gz", None),
            P("gz"),
            P(("gx", "gy", "gz"), None),
        ),
        out_specs=(
            P("gx", "gy", "gz"),
            P("gx", "gy", "gz"),
            P(("gx", "gy", "gz"), None, None, None, None, None),
        ),
        check_vma=False,
    )
```

time: 164 us -> 168 us (1.024)
  blocking collectives: 121 us -> 13.3 us
  waiting for transfers between devices: 0.01 us -> 90.4 us
  starting transfers between devices: 13.7 us -> 27.5 us
  local copies, waits for them, and re-layouts: 5.67 us -> 16.2 us
  Pallas kernels: 21.7 us -> 19 us
    all_to_all x1 -> x0, blocking collectives: 108 us -> none  [local(): lax.all_to_all(outgoing.reshape(group, capacity, 8, 128), ('gy', 'gz'), s...]
    all_to_all x0 -> x1, waiting for transfers between devices: none -> 90.4 us  [local(): lax.all_to_all(outgoing.reshape(group, capacity, 8, 128), ('gy', 'gz'), s...]
    all_to_all x0 -> x1, starting transfers between devices: none -> 12 us  [local(): lax.all_to_all(outgoing.reshape(group, capacity, 8, 128), ('gy', 'gz'), s...]
    unnamed x23 -> x35, local copies, waits for them, and re-layouts: 5.15 us -> 15.7 us
    pallas_call x1, Pallas kernels: 4.56 us -> 2.2 us  [local(): pl.pallas_call(last_kernel, in_specs=[s, s, s, v, v, v, v, v], out_specs=...]
    ppermute x5, starting transfers between devices: 13.7 us -> 15.5 us  [shift(): lax.ppermute(value, axis, [(i, i + by) for i in range(count) if 0 <= i +...]
  transfers between devices with their start and end apart: 5 -> 6, of which waited for: 0 -> 1; matrix products, arithmetic and copies ran while one was open for 0% -> 0% of each run, Pallas kernels for 8% -> 6%
where the time goes in v2:
time: 168 us
  waiting for transfers between devices  90.4 us (54%)
  starting transfers between devices  27.5 us (16%)
  Pallas kernels  19 us (11%)
  local copies, waits for them, and re-layouts  16.2 us (10%)
  blocking collectives  13.3 us (8%)
    all_to_all x1, waiting for transfers between devices, local(): lax.all_to_all(outgoing.reshape(group, capacity, 8, 128), ('gy', 'gz'), s...  90.4 us
    unnamed x35, local copies, waits for them, and re-layouts  15.7 us
    ppermute x5, starting transfers between devices, shift(): lax.ppermute(value, axis, [(i, i + by) for i in range(count) if 0 <= i +...  15.5 us
    all_gather x1, blocking collectives, local(): gathered = lax.all_gather(message, 'gz')  13.3 us
    all_to_all x1, starting transfers between devices, local(): lax.all_to_all(outgoing.reshape(group, capacity, 8, 128), ('gy', 'gz'), s...  12 us
    pallas_call x1, Pallas kernels, local(): pl.pallas_call(head_kernel, grid=grid, in_specs=[s, s, whole((1, 128)), n...  4.68 us
    pallas_call x1, Pallas kernels, local(): pl.pallas_call(main_kernel, grid=grid, in_specs=[whole((32, 128)), nodes,...  3.75 us
    pallas_call x1, Pallas kernels, local(): pl.pallas_call(output_kernel, grid=grid, in_specs=[s, s, s, whole((1, 128...  3.56 us
  transfers between devices with their start and end apart: 6, of which 1 were waited for; matrix products, arithmetic and copies ran while one was open for 0% of the time, Pallas kernels for 6%

profile of v2, /device:TPU:8, one launch (start us, length us, event | category | flops | bytes accessed | tf_op | source)
XLA Modules:
  0.0 167.6 jit_solution(15442962657779253699)
XLA Ops:
  0.7 0.0 copy-start.11
  0.7 4.7 %head.1 = (f32[128,256]{1,0:T(8,128)}, f32[128,256]{1,0:T(8,128)}, f32[128,256]{1,0:T(8,128)}) custom-call(s32[1]{0:T(128)} %bitcast.1.rank_ref.rank_x_ref, f32[16,16]{1,0:T(8,128)} %fx_ref.1, f32[1,128]{1,0:T(1,128)} %bitcast.13, f32[32,128,256]{2,1,0:T(8,128)} %x_ref.5), custom_call_target="tpu_custom_call" | custom-call | flops 2097152 | bytes 4194304 | tf_op jit(solution)/shard_map/head/pallas_call | solution.py:285
  5.4 1.3 collective-permute-start
  6.7 4.6 %collective-permute-start.1 = (f32[128,256]{1,0:T(8,128)}, f32[128,256]{1,0:T(8,128)S(1)}, u32[]{:S(2)}, u32[]{:S(2)}) collective-permute-start(f32[128,256]{1,0:T(8,128)} %get-tuple-element.21), channel_id=1, source_target_pairs={{0,64},{64,128},{128,192},{1,65},{65,129},{129,193},{2,66},{66,130... | collective-permute-start | bytes 393224 | tf_op jit(solution)/shard_map/ppermute | solution.py:266
  11.3 0.1 dynamic_slice.3
  11.3 0.2 slice.6
  11.6 0.2 slice.7
  11.8 2.1 %table.1 = (bf16[256,256]{1,0:T(8,128)(2,1)S(1)}, bf16[256,256]{1,0:T(8,128)(2,1)S(1)}, f32[8,128]{1,0:T(8,128)S(1)}, bf16[128,256]{1,0:T(8,128)(2,1)S(1)}, bf16...) custom-call(s32[1]{0:T(128)} %bitcast.rank_ref, s32[1]{0:T(128)} %bitcast.1.rank_ref.rank_x_ref, f32[2048]{0:T(1024)S(1)} %copy-done.13, ...), custom_call_target="tpu_custom_call" | custom-call | flops 100663296 | bytes 1048576 | tf_op jit(solution)/shard_map/table/pallas_call | solution.py:300
  14.0 0.6 copy-done.8
  14.5 0.2 convert_reduce_fusion
  14.8 0.6 copy-done.3
  15.5 0.0 copy-done.6
  15.5 1.8 %close.1 = f32[136,256]{1,0:T(8,128)} custom-call(f32[16]{0:T(128)} %g_ref.7, f32[32,128]{1,0:T(8,128)} %copy-done.8, f32[128,256]{1,0:T(8,128)} %get-tuple-element.27.own_ref, f32[128,256]{1,0:T(8,128)} %copy-done.3, f32[128,256]{1,0:T(8,128)} %copy-done.6), custom_call_target="tpu_custom_call" | custom-call | tf_op jit(solution)/shard_map/close/pallas_call | solution.py:316
  17.3 3.4 %collective-permute-start.2 = (f32[136,256]{1,0:T(8,128)}, f32[136,256]{1,0:T(8,128)S(1)}, u32[]{:S(2)}, u32[]{:S(2)}) collective-permute-start(f32[136,256]{1,0:T(8,128)} %close.1), channel_id=1, source_target_pairs={{0,64},{64,128},{128,192},{1,65},{65,129},{129,193},{2,66},{66,130... | collective-permute-start | bytes 417800 | tf_op jit(solution)/shard_map/ppermute | solution.py:266
  20.7 4.9 %collective-permute-start.3 = (f32[136,256]{1,0:T(8,128)}, f32[136,256]{1,0:T(8,128)S(1)}, u32[]{:S(2)}, u32[]{:S(2)}) collective-permute-start(f32[136,256]{1,0:T(8,128)} %close.1), channel_id=1, source_target_pairs={{0,128},{64,192},{1,129},{65,193},{2,130},{66,194},{3,131},{67,195... | collective-permute-start | bytes 417800 | tf_op jit(solution)/shard_map/ppermute | solution.py:266
  25.7 1.3 collective-permute-start.4
  27.0 0.0 copy-start
  27.0 2.2 %copy-done = f32[32,128,256]{2,1,0:T(8,128)S(1)} copy-done((f32[32,128,256]{2,1,0:T(8,128)S(1)}, f32[32,128,256]{2,1,0:T(8,128)}, u32[]{:S(2)}) %copy-start) | copy-done | bytes 4194328
  29.2 0.9 copy-done.4
  30.1 0.9 copy-done.7
  31.0 0.7 copy-done.9
  31.7 3.8 %main.1 = (f32[16,128,128]{2,1,0:T(8,128)S(1)}, f32[16,128,128]{2,1,0:T(8,128)S(1)}, f32[128,128]{1,0:T(8,128)S(1)}) custom-call(f32[32,128]{1,0:T(8,128)S(1)} %copy-done.9, f32[32,128,256]{2,1,0:T(8,128)S(1)} %copy-done, f32[128,256]{1,0:T(8,128)S(1)} %copy-done.4, f32[128,256]{1,0:T(8,128)S(1)} %copy-done.7, ...), custom_call_target="tpu_custom_call" | custom-call | flops 805306368 | bytes 10485760 | tf_op jit(solution)/shard_map/main/pallas_call | solution.py:325
  35.5 0.8 carry.1
  36.4 13.3 %all-gather = f32[1024,128]{1,0:T(8,128)S(1)} all-gather(f32[128,128]{1,0:T(8,128)S(1)} %get-tuple-element.31), channel_id=2, replica_groups=mesh['gx'=4,'gy'=8,'gz'=8] {'gz'}, dimensions={0}, use_global_device_ids=true | all-gather | bytes 589824 | tf_op jit(solution)/shard_map/all_gather | solution.py:352
  49.7 2.2 %last.1 = f32[1024,8,128]{2,1,0:T(8,128)S(1)} custom-call(s32[1]{0:T(128)} %bitcast.rank_ref, f32[16]{0:T(128)S(1)} %copy-done.11, s32[512]{0:T(512)S(1)} %multiply_add_fusion.place_ref, f32[16,128,128]{2,1,0:T(8,128)S(1)} %get-tuple-element.26.dz_ref, f32[16,128,128]{2,1,0:T(8,128)S(1)} %get-tuple-element.34.cz_ref, ...), custom_call_target="tpu_custom_call" | custom-call | tf_op jit(solution)/shard_map/last/pallas_call | solution.py:361
  51.9 2.0 %copy-done.2 = f32[1024,8,128]{2,1,0:T(8,128)} copy-done((f32[1024,8,128]{2,1,0:T(8,128)}, f32[1024,8,128]{2,1,0:T(8,128)S(1)}, u32[]{:S(2)}) %copy-start.2) | copy-done | bytes 4194328
  53.9 12.0 %all-to-all-start = ((f32[64,16,8,128]{3,2,1,0:T(8,128)}), f32[64,16,8,128]{3,2,1,0:T(8,128)}, u32[]{:S(2)}, u32[]{:S(2)}) async-start(f32[64,16,8,128]{3,2,1,0:T(8,128)} %bitcast.10), calls=%async_computation | async-start | bytes 8388608 | tf_op jit(solution)/shard_map/all_to_all | solution.py:369
  66.0 0.0 copy-start.1
  66.0 2.2 %copy-done.1 = f32[32,128,256]{2,1,0:T(8,128)S(1)} copy-done((f32[32,128,256]{2,1,0:T(8,128)S(1)}, f32[32,128,256]{2,1,0:T(8,128)}, u32[]{:S(2)}) %copy-start.1) | copy-done | bytes 4194328
  68.2 3.6 %output.1 = (f32[16,128,256]{2,1,0:T(8,128)}, f32[16,128,128]{2,1,0:T(8,128)}) custom-call(s32[1]{0:T(128)} %bitcast.rank_ref, s32[1]{0:T(128)} %bitcast.1.rank_ref.rank_x_ref, f32[16]{0:T(128)S(1)} %copy-done.11, f32[1,128]{1,0:T(1,128)S(1)} %bitcast.15, f32[32,128,256]{2,1,0:T(8,128)S(1)} %copy-done.1, f32[128,256]{1,0:T(8,128)S(1)} %copy-done.5, ...), custom_call_target="tpu_custom_call" | custom-call | flops 1048576 | bytes 8388608 | tf_op jit(solution)/shard_map/output/pallas_call | solution.py:372
  71.7 90.4 %all-to-all-done = f32[64,16,8,128]{3,2,1,0:T(8,128)} async-done(((f32[64,16,8,128]{3,2,1,0:T(8,128)}), f32[64,16,8,128]{3,2,1,0:T(8,128)}, u32[]{:S(2)}, u32[]{:S(2)}) %all-to-all-start) | async-done | bytes 4194336 | tf_op jit(solution)/shard_map/all_to_all | solution.py:369
  162.1 5.5 %copy.12 = f32[1,64,16,2,4,128]{5,4,3,2,1,0:T(4,128)} copy(f32[1,64,16,2,4,128]{5,4,3,2,1,0:T(4,128)} %bitcast.9) | data formatting | bytes 8388608
  (28 shorter events, 0.1 us)
Async XLA Ops:
  0.6 11.2 %copy-start.12 = (f32[128]{0:T(128)S(1)}, f32[128]{0:T(128)}, u32[]{:S(2)}) copy-start(f32[128]{0:T(128)} %param.9) | copy-start | bytes 1540
  0.6 11.2 %copy-start.10 = (f32[16,16]{1,0:T(8,128)S(1)}, f32[16,16]{1,0:T(8,128)}, u32[]{:S(2)}) copy-start(f32[16,16]{1,0:T(8,128)} %fx_ref.1) | copy-start | bytes 3076
  0.7 10.6 %copy-start.13 = (f32[2048]{0:T(1024)S(1)}, f32[2048]{0:T(1024)}, u32[]{:S(2)}) copy-start(f32[2048]{0:T(1024)} %h_ref.1) | copy-start | bytes 24580
  0.7 11.1 %copy-start.15 = (f32[128]{0:T(128)S(1)}, f32[128]{0:T(128)}, u32[]{:S(2)}) copy-start(f32[128]{0:T(128)} %param.14) | copy-start | bytes 1540
  0.7 11.1 %copy-start.14 = (f32[128,128]{1,0:T(8,128)S(1)}, f32[128,128]{1,0:T(8,128)}, u32[]{:S(2)}) copy-start(f32[128,128]{1,0:T(8,128)} %f_ref.3) | copy-start | bytes 196612
  0.7 13.9 %copy-start.16 = (s32[512,1]{0,1:T(1,128)S(1)}, s32[512,1]{0,1:T(1,128)}, u32[]{:S(2)}) copy-start(s32[512,1]{0,1:T(1,128)} %param.15) | copy-start | bytes 6148
  0.7 34.8 %copy-start.11 = (f32[16]{0:T(128)S(1)}, f32[16]{0:T(128)}, u32[]{:S(2)}) copy-start(f32[16]{0:T(128)} %g_ref.7) | copy-start | bytes 196
  5.4 9.4 %collective-permute-start = (f32[128,256]{1,0:T(8,128)}, f32[128,256]{1,0:T(8,128)S(1)}, u32[]{:S(2)}, u32[]{:S(2)}) collective-permute-start(f32[128,256]{1,0:T(8,128)} %get-tuple-element.19), channel_id=1, source_target_pairs={{64,0},{128,64},{192,128},{65,1},{129,65},{193,129},{66,2},{130,66... | collective-permute-start | bytes 393224 | tf_op jit(solution)/shard_map/ppermute | solution.py:266
  6.7 8.1 %collective-permute-start.1 = (f32[128,256]{1,0:T(8,128)}, f32[128,256]{1,0:T(8,128)S(1)}, u32[]{:S(2)}, u32[]{:S(2)}) collective-permute-start(f32[128,256]{1,0:T(8,128)} %get-tuple-element.21), channel_id=1, source_target_pairs={{0,64},{64,128},{128,192},{1,65},{65,129},{129,193},{2,66},{66,130... | collective-permute-start | bytes 393224 | tf_op jit(solution)/shard_map/ppermute | solution.py:266
  13.9 0.6 copy-start.8
  14.8 0.7 copy-start.3
  14.8 0.7 copy-start.6
  17.3 18.2 %collective-permute-start.2 = (f32[136,256]{1,0:T(8,128)}, f32[136,256]{1,0:T(8,128)S(1)}, u32[]{:S(2)}, u32[]{:S(2)}) collective-permute-start(f32[136,256]{1,0:T(8,128)} %close.1), channel_id=1, source_target_pairs={{0,64},{64,128},{128,192},{1,65},{65,129},{129,193},{2,66},{66,130... | collective-permute-start | bytes 417800 | tf_op jit(solution)/shard_map/ppermute | solution.py:266
  20.7 14.8 %collective-permute-start.3 = (f32[136,256]{1,0:T(8,128)}, f32[136,256]{1,0:T(8,128)S(1)}, u32[]{:S(2)}, u32[]{:S(2)}) collective-permute-start(f32[136,256]{1,0:T(8,128)} %close.1), channel_id=1, source_target_pairs={{0,128},{64,192},{1,129},{65,193},{2,130},{66,194},{3,131},{67,195... | collective-permute-start | bytes 417800 | tf_op jit(solution)/shard_map/ppermute | solution.py:266
  25.7 9.8 %collective-permute-start.4 = (f32[136,256]{1,0:T(8,128)}, f32[136,256]{1,0:T(8,128)S(1)}, u32[]{:S(2)}, u32[]{:S(2)}) collective-permute-start(f32[136,256]{1,0:T(8,128)} %close.1), channel_id=1, source_target_pairs={{0,192},{1,193},{2,194},{3,195},{4,196},{5,197},{6,198},{7,199},{8... | collective-permute-start | bytes 417800 | tf_op jit(solution)/shard_map/ppermute | solution.py:266
  27.0 2.2 %copy-start = (f32[32,128,256]{2,1,0:T(8,128)S(1)}, f32[32,128,256]{2,1,0:T(8,128)}, u32[]{:S(2)}) copy-start(f32[32,128,256]{2,1,0:T(8,128)} %x_ref.5) | copy-start | bytes 12582916
  29.2 0.9 copy-start.4
  30.1 0.9 copy-start.7
  31.0 0.7 copy-start.9
  51.9 2.0 %copy-start.2 = (f32[1024,8,128]{2,1,0:T(8,128)}, f32[1024,8,128]{2,1,0:T(8,128)S(1)}, u32[]{:S(2)}) copy-start(f32[1024,8,128]{2,1,0:T(8,128)S(1)} %last.1) | copy-start | bytes 12582916
  53.9 12.0 %copy-start.5 = (f32[128,256]{1,0:T(8,128)S(1)}, f32[128,256]{1,0:T(8,128)}, u32[]{:S(2)}) copy-start(f32[128,256]{1,0:T(8,128)} %copy-done.3) | copy-start | bytes 393220
  53.9 108.1 %all-to-all-start = ((f32[64,16,8,128]{3,2,1,0:T(8,128)}), f32[64,16,8,128]{3,2,1,0:T(8,128)}, u32[]{:S(2)}, u32[]{:S(2)}) async-start(f32[64,16,8,128]{3,2,1,0:T(8,128)} %bitcast.10), calls=%async_computation | async-start | bytes 8388608 | tf_op jit(solution)/shard_map/all_to_all | solution.py:369
  66.0 2.2 %copy-start.1 = (f32[32,128,256]{2,1,0:T(8,128)S(1)}, f32[32,128,256]{2,1,0:T(8,128)}, u32[]{:S(2)}) copy-start(f32[32,128,256]{2,1,0:T(8,128)} %x_ref.5) | copy-start | bytes 12582916

commit v3 on v2

--- a/solution.py
+++ b/solution.py
@@ -20,7 +20,7 @@
     return pl.CostEstimate(flops=flops, bytes_accessed=moved, transcendentals=0)
 
 
-def params(mib=16):
+def params(mib=56):
     return pltpu.CompilerParams(vmem_limit_bytes=mib << 20)
 
 
@@ -31,22 +31,31 @@
     return after / total, own / total, 0.5 * own, 0.5 * after
 
 
-def head_kernel(rank_ref, f_ref, h_ref, x_ref, first_ref, last_ref, out_ref):
-    rows_of = weights_x(rank_ref, h_ref)
-    weight = lambda i, k: rows_of[i][0:1, (2 * k) % 128 : (2 * k) % 128 + 1]
-    far_before = jnp.where(rank_ref[0] > 0, weight(3, -1), 0.0)
-    before = -f_ref[15, 0] * far_before * weight(1, -1)
-    total = None
-    for j in range(16):
-        v = f_ref[15, j] * weight(2, j)
-        if j < 15:
-            v = v + f_ref[15, j + 1] * weight(3, j)
-        term = (before - v * weight(0, j)) * x_ref[2 * j] + v * x_ref[2 * j + 1]
-        total = term if total is None else total + term
-        before = -v * weight(1, j)
-    out_ref[...] = total
-    first_ref[...] = x_ref[0]
-    last_ref[...] = x_ref[31] - weight(0, 15) * x_ref[30]
+def head_kernel(rank_ref, f_ref, h_ref, x_ref, first_ref, last_ref, out_ref, w_ref):
+    @pl.when(pl.program_id(0) == 0)
+    def _():
+        rows_of = weights_x(rank_ref, h_ref)
+        weight = lambda i, k: jnp.broadcast_to(rows_of[i][:, (2 * k) % 128 : (2 * k) % 128 + 1], (8, 128))
+        far_before = jnp.where(rank_ref[0] > 0, weight(3, -1), 0.0)
+        before = -f_ref[15, 0] * far_before * weight(1, -1)
+        for j in range(16):
+            v = f_ref[15, j] * weight(2, j)
+            if j < 15:
+                v = v + f_ref[15, j + 1] * weight(3, j)
+            w_ref[2 * j] = before - v * weight(0, j)
+            w_ref[2 * j + 1] = v
+            before = -v * weight(1, j)
+        w_ref[32] = weight(0, 15)
+
+    for r in range(x_ref.shape[1] // 8):
+        for half in range(2):
+            at = (slice(8 * r, 8 * r + 8), slice(128 * half, 128 * half + 128))
+            total = w_ref[0] * x_ref[(0, *at)]
+            for x in range(1, 32):
+                total = total + w_ref[x] * x_ref[(x, *at)]
+            out_ref[at] = total
+            first_ref[at] = x_ref[(0, *at)]
+            last_ref[at] = x_ref[(31, *at)] - w_ref[32] * x_ref[(30, *at)]
 
 
 def close_kernel(g_ref, row_ref, own_ref, right_ref, left_ref, out_ref):
@@ -226,34 +235,20 @@
     out_ref[...] = message
 
 
-def last_kernel(
-    rank_ref, g_ref, place_ref, dz_ref, cz_ref, plane_ref, all_ref, row_ref, out_ref
-):
-    rank = rank_ref[0]
+def place_kernel(g_ref, place_ref, dz_ref, cz_ref, plane_ref, message_ref, row_ref, out_ref, note_ref):
+    note_ref[0:128] = message_ref[...]
+    note_ref[128:136] = row_ref[...]
 
     def clear(i, _):
         out_ref[pl.ds(pl.multiple_of(i * 16, 16), 16)] = jnp.zeros((16, 8, 128), F32)
         return 0
 
     lax.fori_loop(0, out_ref.shape[0] // 16, clear, 0)
-    carry = jnp.zeros((128, 128), F32)
-    for r in range(7):
-        entering = carry * all_ref[r, 0:1, 50:51] + pltpu.roll(all_ref[r], 96, 1)
-        entering = entering + all_ref[r, 0:1, 48:49] * all_ref[r + 1]
-        if r > 0:
-            entering = entering + all_ref[r, 0:1, 49:50] * pltpu.roll(all_ref[r - 1], 112, 1)
-        carry = jnp.where(r < rank, entering, carry)
-    right = jnp.where(rank < 7, all_ref[jnp.minimum(rank + 1, 7)], 0.0)
-    left = pltpu.roll(all_ref[jnp.maximum(rank - 1, 0)], 112, 1)
-    d_right, c_right, c_left, gain = (row_ref[i : i + 1, :] for i in range(4))
-    spread = lambda value, k: jnp.broadcast_to(value[:, k : k + 1], (128, 128))
     top = lax.broadcasted_iota(jnp.int32, (8, 128), 0) < 4
     for k in range(16):
         g = g_ref[k]
-        right_k = spread(right, k)
-        detail = dz_ref[k] + g * plane_ref[:, 0:128] + right_k * d_right
-        coarse = cz_ref[k] + g * plane_ref[:, 128:256] + right_k * c_right
-        coarse = coarse + spread(left, k) * c_left + spread(carry, k) * gain
+        detail = dz_ref[k] + g * plane_ref[:, 0:128]
+        coarse = cz_ref[k] + g * plane_ref[:, 128:256]
         for i in range(16):
             c8, d8 = coarse[8 * i : 8 * i + 8], detail[8 * i : 8 * i + 8]
             block = 32 * k + 2 * i
@@ -261,9 +256,69 @@
             out_ref[place_ref[block + 1]] = jnp.where(top, pltpu.roll(c8, 4, 0), d8)
 
 
+def lines_kernel(rank_ref, rank_y_ref, place_ref, all_ref, out_ref, z_ref):
+    rank = rank_ref[0]
+    columns = lambda r: all_ref[r, 0:128, :]
+    carry = jnp.zeros((128, 128), F32)
+    for r in range(7):
+        entering = carry * all_ref[r, 0:1, 50:51] + pltpu.roll(columns(r), 96, 1)
+        entering = entering + all_ref[r, 0:1, 48:49] * columns(r + 1)
+        if r > 0:
+            entering = entering + all_ref[r, 0:1, 49:50] * pltpu.roll(columns(r - 1), 112, 1)
+        carry = jnp.where(r < rank, entering, carry)
+    right = jnp.where(rank < 7, columns(jnp.minimum(rank + 1, 7)), 0.0)
+    left = columns(jnp.maximum(rank - 1, 0))
+    wide = lax.broadcasted_iota(jnp.int32, (128, 128), 1)
+    z_ref[...] = jnp.where(
+        wide < 16, carry, jnp.where(wide < 32, pltpu.roll(right, 16, 1), pltpu.roll(left, 16, 1))
+    )
+    out_ref[...] = jnp.zeros(out_ref.shape, F32)
+    lane = lax.broadcasted_iota(jnp.int32, (8, 128), 1)
+
+    def body(pair, _):
+        k, i = pair // 16, pair % 16
+        piece = z_ref[pl.ds(pl.multiple_of(i * 8, 8), 8), :]
+        for odd in range(2):
+            place = place_ref[2 * pair + odd]
+            to, slot = place // 16, place % 16
+            ahead_y = (to // 8 - rank_y_ref[0] + 8) % 8
+            ahead_z = (to % 8 - rank + 8) % 8
+            moved = pltpu.roll(piece, (slot - k + 128) % 128, 1)
+            mine = ((lane % 16) == slot) & (lane < 48)
+            part = slice(4 * odd, 4 * odd + 4)
+            out_ref[ahead_y, ahead_z] = jnp.where(mine[part], moved[part], out_ref[ahead_y, ahead_z])
+        return 0
+
+    lax.fori_loop(0, 256, body, 0)
+
+
+def receive_kernel(rank_ref, rank_y_ref, tile_ref, line_ref, all_ref, out_ref):
+    top = lax.broadcasted_iota(jnp.int32, (8, 128), 0) < 4
+    for q in range(8):
+        row = lambda i: jnp.broadcast_to(all_ref[q, 128 + i : 129 + i, :], (8, 128))
+        of_carry = jnp.where(top, row(3), 0.0)
+        of_right = jnp.where(top, row(1), row(0))
+        of_left = jnp.where(top, row(2), 0.0)
+        line = line_ref[(rank_ref[0] - q + 8) % 8, (rank_y_ref[0] - pl.program_id(0) + 8) % 8]
+        lines = jnp.concatenate([line, line], axis=0)
+        spread = lambda lane: jnp.broadcast_to(lines[:, lane : lane + 1], (8, 128))
+        for m in range(16):
+            t = 16 * q + m
+            out_ref[t] = (
+                tile_ref[t] + spread(m) * of_carry + spread(16 + m) * of_right + spread(32 + m) * of_left
+            )
+
+
 def shift(value, axis, by):
     count = lax.axis_size(axis)
     return lax.ppermute(value, axis, [(i, i + by) for i in range(count) if 0 <= i + by < count])
+
+
+def ring(value, axis, by):
+    count = lax.axis_size(axis)
+    if by == 0:
+        return value
+    return lax.ppermute(value, axis, [(i, (i + by) % count) for i in range(count)])
 
 
 def local(
@@ -271,6 +326,7 @@
 ):
     rank_x = lax.axis_index("gx").astype(jnp.int32).reshape(1)
     rank_z = lax.axis_index("gz").astype(jnp.int32).reshape(1)
+    rank_y = lax.axis_index("gy").astype(jnp.int32).reshape(1)
     plane = jax.ShapeDtypeStruct((128, 256), F32)
     s, v = spec(SMEM), spec(VMEM)
 
@@ -288,6 +344,8 @@
         in_specs=[s, s, whole((1, 128)), nodes],
         out_specs=[thin, thin, thin],
         out_shape=[plane, plane, plane],
+        scratch_shapes=[VMEM((33, 8, 128), F32)],
+        compiler_params=params(),
         cost_estimate=cost(64 * 32768, 4 << 20),
         name="head",
     )(rank_x, operator_x, space_x, nodal_field)
@@ -318,6 +376,7 @@
         in_specs=[s, v, v, v, v],
         out_specs=v,
         out_shape=jax.ShapeDtypeStruct((136, 256), F32),
+        compiler_params=params(),
         name="close",
     )(persist_x, x_rows, own, right, left)
     one, two, three = (shift(ended, "gx", by) for by in (1, 2, 3))
@@ -349,7 +408,6 @@
         compiler_params=params(),
         name="carry",
     )(persist_x, one, two, three, high, low, rows, columns)
-    gathered = lax.all_gather(message, "gz")
 
     group = lax.axis_size("gy") * lax.axis_size("gz")
     capacity = 16
@@ -358,22 +416,38 @@
     earlier = (targets[None, :] == targets[:, None]) & (positions[None, :] < positions[:, None])
     placed = targets * capacity + jnp.sum(earlier.astype(jnp.int32), axis=1)
 
-    outgoing = pl.pallas_call(
-        last_kernel,
-        in_specs=[s, s, s, v, v, v, v, v],
-        out_specs=v,
-        out_shape=jax.ShapeDtypeStruct((group * capacity, 8, 128), F32),
-        compiler_params=params(),
-        name="last",
-    )(rank_z, persist_x, placed, dz, cz, plane_pass, gathered, rows)
+    outgoing, note = pl.pallas_call(
+        place_kernel,
+        in_specs=[s, s, v, v, v, v, v],
+        out_specs=[v, v],
+        out_shape=[
+            jax.ShapeDtypeStruct((group * capacity, 8, 128), F32),
+            jax.ShapeDtypeStruct((136, 128), F32),
+        ],
+        compiler_params=params(),
+        name="place",
+    )(persist_x, placed, dz, cz, plane_pass, message, rows)
     incoming = lax.all_to_all(
         outgoing.reshape(group, capacity, 8, 128), ("gy", "gz"), split_axis=0, concat_axis=0, tiled=True
     )
+    gathered = lax.all_gather(note, "gz")
+    lines = pl.pallas_call(
+        lines_kernel,
+        in_specs=[s, s, s, v],
+        out_specs=v,
+        out_shape=jax.ShapeDtypeStruct((8, 8, 4, 128), F32),
+        scratch_shapes=[VMEM((128, 128), F32)],
+        compiler_params=params(),
+        cost_estimate=cost(1 << 24, 1 << 20),
+        name="lines",
+    )(rank_z, rank_y, placed, gathered)
+    moved = jnp.stack([ring(lines[by], "gy", by) for by in range(8)])
+    lines_in = jnp.stack([ring(moved[:, by], "gz", by) for by in range(8)])
     detail_x, detail_z = pl.pallas_call(
         output_kernel,
         grid=grid,
         in_specs=[
-            s, s, s, whole((1, 128)), nodes, thin, third, thin, whole((8, 128, 128)), whole((8, 128)),
+            s, s, s, whole((1, 128)), nodes, thin, third, thin, whole((8, 136, 128)), whole((8, 128)),
         ],
         out_specs=[pl.BlockSpec((16, chunk, 256), lambda i: (0, i, 0)), third],
         out_shape=[
@@ -384,7 +458,17 @@
         cost_estimate=cost(1 << 20, 8 << 20),
         name="output",
     )(rank_z, rank_x, persist_x, space_x, nodal_field, right, dz, plane_pass, gathered, rows)
-    received = incoming.reshape(1, group, capacity, 2, LINES, 128)
+    tiles = pl.BlockSpec((128, 8, 128), lambda i: (i, 0, 0))
+    complete = pl.pallas_call(
+        receive_kernel,
+        grid=(group // 8,),
+        in_specs=[s, s, tiles, whole((8, 8, 4, 128)), whole((8, 136, 128))],
+        out_specs=tiles,
+        out_shape=jax.ShapeDtypeStruct((group * capacity, 8, 128), F32),
+        compiler_params=params(),
+        name="receive",
+    )(rank_z, rank_y, incoming.reshape(group * capacity, 8, 128), lines_in, gathered)
+    received = complete.reshape(1, group, capacity, 2, LINES, 128)
     return (detail_x, detail_z, received)
 
 

time: 168 us -> 186 us (1.11); the launches traced: 168 us -> 182 us
  waiting for transfers between devices: 90.4 us -> 44.3 us
  Pallas kernels: 19 us -> 58.1 us
  starting transfers between devices: 27.5 us -> 50.6 us
  local copies, waits for them, and re-layouts: 16.2 us -> 6.05 us
  blocking collectives: 13.3 us -> 21.4 us
    all_to_all x1, waiting for transfers between devices: 90.4 us -> 0.01 us  [local(): lax.all_to_all(outgoing.reshape(group, capacity, 8, 128), ('gy', 'gz'), s...]
    ppermute x0 -> x14, waiting for transfers between devices: none -> 44.2 us  [ring(): lax.ppermute(value, axis, [(i, (i + by) % count) for i in range(count)])]
    pallas_call x1 -> x3, Pallas kernels: 2.2 us -> 35.2 us  [the longest x1 21.1 us: local(): pl.pallas_call(lines_kernel, in_specs=[s, s, s, v], out_specs=v, out_shap...]
    ppermute x0 -> x14, starting transfers between devices: none -> 25.3 us  [ring(): lax.ppermute(value, axis, [(i, (i + by) % count) for i in range(count)])]
    unnamed x35 -> x30, local copies, waits for them, and re-layouts: 15.7 us -> 2.89 us
    all_gather x1, blocking collectives: 13.3 us -> 21.4 us  [local(): gathered = lax.all_gather(note, 'gz')]
    ppermute x5, starting transfers between devices: 15.5 us -> 12.9 us  [shift(): lax.ppermute(value, axis, [(i, i + by) for i in range(count) if 0 <= i +...]
    pallas_call x1, Pallas kernels: 3.75 us -> 6.21 us  [local(): pl.pallas_call(main_kernel, grid=grid, in_specs=[whole((32, 128)), nodes,...]
  transfers between devices with their start and end apart: 6 -> 20, of which waited for: 1 -> 5; matrix products, arithmetic and copies ran while one was open for 0% -> 3% of each run, Pallas kernels for 6% -> 20%
where the time goes in v3:
time: 186 us; the launch traced here: 182 us
  Pallas kernels  58.1 us (31%)
  starting transfers between devices  50.6 us (27%)
  waiting for transfers between devices  44.3 us (24%)
  blocking collectives  21.4 us (12%)
  local copies, waits for them, and re-layouts  6.05 us (3%)
    ppermute x14, waiting for transfers between devices, ring(): lax.ppermute(value, axis, [(i, (i + by) % count) for i in range(count)])  44.2 us
    ppermute x14, starting transfers between devices, ring(): lax.ppermute(value, axis, [(i, (i + by) % count) for i in range(count)])  25.3 us
    all_gather x1, blocking collectives, local(): gathered = lax.all_gather(note, 'gz')  21.4 us
    pallas_call x1, Pallas kernels, local(): pl.pallas_call(lines_kernel, in_specs=[s, s, s, v], out_specs=v, out_shap...  21.1 us
    ppermute x5, starting transfers between devices, shift(): lax.ppermute(value, axis, [(i, i + by) for i in range(count) if 0 <= i +...  12.9 us
    all_to_all x1, starting transfers between devices, local(): lax.all_to_all(outgoing.reshape(group, capacity, 8, 128), ('gy', 'gz'), s...  12.4 us
    pallas_call x1, Pallas kernels, local(): pl.pallas_call(receive_kernel, grid=(group // 8,), in_specs=[s, s, tiles,...  9.65 us
    pallas_call x1, Pallas kernels, local(): pl.pallas_call(main_kernel, grid=grid, in_specs=[whole((32, 128)), nodes,...  6.21 us
  transfers between devices with their start and end apart: 20, of which 5 were waited for; matrix products, arithmetic and copies ran while one was open for 3% of the time, Pallas kernels for 20%

profile of v3, /device:TPU:8, one launch (start us, length us, event | category | flops | bytes accessed | tf_op | source)
XLA Modules:
  0.0 182.1 jit_solution(5266631922337045828)
XLA Ops:
  0.6 4.3 %head.1 = (f32[128,256]{1,0:T(8,128)}, f32[128,256]{1,0:T(8,128)}, f32[128,256]{1,0:T(8,128)}) custom-call(s32[1]{0:T(128)} %bitcast.1.rank_ref.rank_x_ref, f32[16,16]{1,0:T(8,128)} %fx_ref.1, f32[1,128]{1,0:T(1,128)} %bitcast.83, f32[32,128,256]{2,1,0:T(8,128)} %x_ref.5), custom_call_target="tpu_custom_call" | custom-call | flops 2097152 | bytes 4194304 | tf_op jit(solution)/shard_map/head/pallas_call | solution.py:341
  4.9 1.3 collective-permute-start
  6.2 4.6 %collective-permute-start.1 = (f32[128,256]{1,0:T(8,128)}, f32[128,256]{1,0:T(8,128)S(1)}, u32[]{:S(2)}, u32[]{:S(2)}) collective-permute-start(f32[128,256]{1,0:T(8,128)} %get-tuple-element.23), channel_id=1, source_target_pairs={{0,64},{64,128},{128,192},{1,65},{65,129},{129,193},{2,66},{66,130... | collective-permute-start | bytes 393224 | tf_op jit(solution)/shard_map/ppermute | solution.py:314
  11.6 0.8 slice.55
  13.1 3.0 %table.1 = (bf16[256,256]{1,0:T(8,128)(2,1)}, bf16[256,256]{1,0:T(8,128)(2,1)}, f32[8,128]{1,0:T(8,128)}, bf16[128,256]{1,0:T(8,128)(2,1)}, bf16[128,256]{1,0:T(8,128)(2,1)}, /*index=5*/f32[32,128]{1,0:T(8,128)}) custom-call(s32[1]{0:T(128)} %bitcast.rank_ref, s32[1]{0:T(128)} %bitcast.1.rank_ref.rank_x_ref, f32[2048]{0:T(1024)} %h_ref.1, ...), custom_call_target="tpu_custom_call" | custom-call | flops 100663296 | bytes 1048576 | tf_op jit(solution)/shard_map/table/pallas_call | solution.py:358
  17.1 1.8 close.1
  18.9 3.0 %collective-permute-start.4 = (f32[136,256]{1,0:T(8,128)}, f32[136,256]{1,0:T(8,128)S(1)}, u32[]{:S(2)}, u32[]{:S(2)}) collective-permute-start(f32[136,256]{1,0:T(8,128)} %close.1), channel_id=1, source_target_pairs={{0,192},{1,193},{2,194},{3,195},{4,196},{5,197},{6,198},{7,199},{8... | collective-permute-start | bytes 417800 | tf_op jit(solution)/shard_map/ppermute | solution.py:314
  21.9 2.6 %collective-permute-start.3 = (f32[136,256]{1,0:T(8,128)}, f32[136,256]{1,0:T(8,128)S(1)}, u32[]{:S(2)}, u32[]{:S(2)}) collective-permute-start(f32[136,256]{1,0:T(8,128)} %close.1), channel_id=1, source_target_pairs={{0,128},{64,192},{1,129},{65,193},{2,130},{66,194},{3,131},{67,195... | collective-permute-start | bytes 417800 | tf_op jit(solution)/shard_map/ppermute | solution.py:314
  24.5 1.4 collective-permute-start.2
  26.5 6.2 %main.1 = (f32[16,128,128]{2,1,0:T(8,128)}, f32[16,128,128]{2,1,0:T(8,128)}, f32[128,128]{1,0:T(8,128)}) custom-call(f32[32,128]{1,0:T(8,128)} %get-tuple-element.22.x_row_ref.row_ref, f32[32,128,256]{2,1,0:T(8,128)} %x_ref.5, f32[128,256]{1,0:T(8,128)} %copy-done, f32[128,256]{1,0:T(8,128)} %copy-done.1, bf16[128,256]{1,0:T(8,128)(2,1)} %get-tuple-element.24.x_high_ref, ...), custom_call_target="tpu_custom_call" | custom-call | flops 805306368 | bytes 10485760 | tf_op jit(solution)/shard_map/main/pallas_call | solution.py:384
  33.5 2.1 %carry.1 = (f32[128,256]{1,0:T(8,128)}, f32[128,128]{1,0:T(8,128)}) custom-call(f32[16]{0:T(128)} %g_ref.7, f32[136,256]{1,0:T(8,128)} %copy-done.5, f32[136,256]{1,0:T(8,128)} %copy-done.4, f32[136,256]{1,0:T(8,128)} %copy-done.3, bf16[256,256]{1,0:T(8,128)(2,1)} %get-tuple-element.26.high_ref, bf16[256,256]{1,0:T(8,128)(2,1)} %get-tuple-element.27.low_ref, ...), custom_call_target="tpu_custom_call" | custom-call | tf_op jit(solution)/shard_map/carry/pallas_call | solution.py:403
  35.7 4.4 %place.1 = (f32[1024,8,128]{2,1,0:T(8,128)}, f32[136,128]{1,0:T(8,128)}) custom-call(f32[16]{0:T(128)} %g_ref.7, s32[512]{0:T(512)} %multiply_add_fusion.place_ref, f32[16,128,128]{2,1,0:T(8,128)} %get-tuple-element.28.dz_ref, f32[16,128,128]{2,1,0:T(8,128)} %get-tuple-element.33.cz_ref, f32[128,256]{1,0:T(8,128)} %get-tuple-element.32.plane_ref, ...), custom_call_target="tpu_custom_call" | custom-call | tf_op jit(solution)/shard_map/place/pallas_call | solution.py:419
  40.0 12.4 %all-to-all-start = ((f32[64,16,8,128]{3,2,1,0:T(8,128)}), f32[64,16,8,128]{3,2,1,0:T(8,128)}, u32[]{:S(2)}, u32[]{:S(2)}) async-start(f32[64,16,8,128]{3,2,1,0:T(8,128)} %bitcast.80), calls=%async_computation | async-start | bytes 8388608 | tf_op jit(solution)/shard_map/all_to_all | solution.py:430
  52.5 21.4 %all-gather = f32[1088,128]{1,0:T(8,128)} all-gather(f32[136,128]{1,0:T(8,128)S(1)} %copy-done.6), channel_id=2, replica_groups=mesh['gx'=4,'gy'=8,'gz'=8] {'gz'}, dimensions={0}, use_global_device_ids=true | all-gather | bytes 626688 | tf_op jit(solution)/shard_map/all_gather | solution.py:433
  73.9 21.1 %lines.1 = f32[8,8,4,128]{3,2,1,0:T(4,128)} custom-call(s32[1]{0:T(128)} %bitcast.rank_ref, s32[1]{0:T(128)} %bitcast.8.rank_y_ref, s32[512]{0:T(512)} %multiply_add_fusion.place_ref, f32[8,136,128]{2,1,0:T(8,128)} %bitcast.76), custom_call_target="tpu_custom_call" | custom-call | flops 16777216 | bytes 1048576 | tf_op jit(solution)/shard_map/lines/pallas_call | solution.py:434
  95.0 0.8 slice_bitcast_fusion.8
  95.9 4.2 %collective-permute-start.5 = (f32[8,4,128]{2,1,0:T(4,128)S(1)}, f32[8,4,128]{2,1,0:T(4,128)S(1)}, u32[]{:S(2)}, u32[]{:S(2)}) collective-permute-start(f32[8,4,128]{2,1,0:T(4,128)S(1)} %get-tuple-element.52), channel_id=1, source_target_pairs={{0,8},{8,16},{16,24},{24,32},{32,40},{40,48},{48,56},{56,0},{1,9},... | collective-permute-start | bytes 49160 | tf_op jit(solution)/shard_map/ppermute | solution.py:321
  100.7 0.8 collective-permute-start.11
  101.6 1.4 collective-permute-start.10
  103.0 6.3 %collective-permute-start.9 = (f32[8,4,128]{2,1,0:T(4,128)S(1)}, f32[8,4,128]{2,1,0:T(4,128)S(1)}, u32[]{:S(2)}, u32[]{:S(2)}) collective-permute-start(f32[8,4,128]{2,1,0:T(4,128)S(1)} %get-tuple-element.48), channel_id=1, source_target_pairs={{0,40},{8,48},{16,56},{24,0},{32,8},{40,16},{48,24},{56,32},{1,41}... | collective-permute-start | bytes 49160 | tf_op jit(solution)/shard_map/ppermute | solution.py:321
  109.5 5.4 %output.1 = (f32[16,128,256]{2,1,0:T(8,128)}, f32[16,128,128]{2,1,0:T(8,128)}) custom-call(s32[1]{0:T(128)} %bitcast.rank_ref, s32[1]{0:T(128)} %bitcast.1.rank_ref.rank_x_ref, f32[16]{0:T(128)} %g_ref.7, f32[1,128]{1,0:T(1,128)} %bitcast.85, f32[32,128,256]{2,1,0:T(8,128)} %x_ref.5, f32[128,256]{1,0:T(8,128)} %copy-done, ...), custom_call_target="tpu_custom_call" | custom-call | flops 1048576 | bytes 8388608 | tf_op jit(solution)/shard_map/output/pallas_call | solution.py:446
  115.0 28.3 %collective-permute-done.5 = f32[8,4,128]{2,1,0:T(4,128)S(1)} collective-permute-done((f32[8,4,128]{2,1,0:T(4,128)S(1)}, f32[8,4,128]{2,1,0:T(4,128)S(1)}, u32[]{:S(2)}, u32[]{:S(2)}) %collective-permute-start.5) | collective-permute-done | bytes 16416 | tf_op jit(solution)/shard_map/ppermute | solution.py:321
  143.2 2.6 %collective-permute-start.6 = (f32[8,4,128]{2,1,0:T(4,128)S(1)}, f32[8,4,128]{2,1,0:T(4,128)S(1)}, u32[]{:S(2)}, u32[]{:S(2)}) collective-permute-start(f32[8,4,128]{2,1,0:T(4,128)S(1)} %get-tuple-element.51), channel_id=1, source_target_pairs={{0,16},{8,24},{16,32},{24,40},{32,48},{40,56},{48,0},{56,8},{1,17}... | collective-permute-start | bytes 49160 | tf_op jit(solution)/shard_map/ppermute | solution.py:321
  145.9 3.2 %collective-permute-done.6 = f32[8,4,128]{2,1,0:T(4,128)S(1)} collective-permute-done((f32[8,4,128]{2,1,0:T(4,128)S(1)}, f32[8,4,128]{2,1,0:T(4,128)S(1)}, u32[]{:S(2)}, u32[]{:S(2)}) %collective-permute-start.6) | collective-permute-done | bytes 16416 | tf_op jit(solution)/shard_map/ppermute | solution.py:321
  149.1 3.3 %collective-permute-start.7 = (f32[8,4,128]{2,1,0:T(4,128)S(1)}, f32[8,4,128]{2,1,0:T(4,128)S(1)}, u32[]{:S(2)}, u32[]{:S(2)}) collective-permute-start(f32[8,4,128]{2,1,0:T(4,128)S(1)} %get-tuple-element.50), channel_id=1, source_target_pairs={{0,24},{8,32},{16,40},{24,48},{32,56},{40,0},{48,8},{56,16},{1,25}... | collective-permute-start | bytes 49160 | tf_op jit(solution)/shard_map/ppermute | solution.py:321
  152.4 4.3 %collective-permute-done.7 = f32[8,4,128]{2,1,0:T(4,128)S(1)} collective-permute-done((f32[8,4,128]{2,1,0:T(4,128)S(1)}, f32[8,4,128]{2,1,0:T(4,128)S(1)}, u32[]{:S(2)}, u32[]{:S(2)}) %collective-permute-start.7) | collective-permute-done | bytes 16416 | tf_op jit(solution)/shard_map/ppermute | solution.py:321
  156.8 1.7 collective-permute-start.18
  158.5 3.0 %collective-permute-start.17 = (f32[8,4,128]{2,1,0:T(4,128)S(1)}, f32[8,4,128]{2,1,0:T(4,128)S(1)}, u32[]{:S(2)}, u32[]{:S(2)}) collective-permute-start(f32[8,4,128]{2,1,0:T(4,128)S(1)} %get-tuple-element.40), channel_id=1, source_target_pairs={{0,6},{1,7},{2,0},{3,1},{4,2},{5,3},{6,4},{7,5},{8,14},{9,15},{10,... | collective-permute-start | bytes 49160 | tf_op jit(solution)/shard_map/ppermute | solution.py:321
  162.0 1.2 collective-permute-start.13
  163.2 3.9 %collective-permute-done.13 = f32[8,4,128]{2,1,0:T(4,128)S(1)} collective-permute-done((f32[8,4,128]{2,1,0:T(4,128)S(1)}, f32[8,4,128]{2,1,0:T(4,128)S(1)}, u32[]{:S(2)}, u32[]{:S(2)}) %collective-permute-start.13) | collective-permute-done | bytes 16416 | tf_op jit(solution)/shard_map/ppermute | solution.py:321
  167.1 4.7 %collective-permute-done.14 = f32[8,4,128]{2,1,0:T(4,128)S(1)} collective-permute-done((f32[8,4,128]{2,1,0:T(4,128)S(1)}, f32[8,4,128]{2,1,0:T(4,128)S(1)}, u32[]{:S(2)}, u32[]{:S(2)}) %collective-permute-start.14) | collective-permute-done | bytes 16416 | tf_op jit(solution)/shard_map/ppermute | solution.py:321
  172.5 9.7 %receive.1 = f32[1024,8,128]{2,1,0:T(8,128)} custom-call(s32[1]{0:T(128)} %bitcast.rank_ref, s32[1]{0:T(128)} %bitcast.8.rank_y_ref, f32[1024,8,128]{2,1,0:T(8,128)} %bitcast.10.tile_ref, f32[8,8,4,128]{3,2,1,0:T(4,128)} %copy-done.2, f32[8,136,128]{2,1,0:T(8,128)} %bitcast.78), custom_call_target="tpu_custom_call" | custom-call | tf_op jit(solution)/shard_map/receive/pallas_call | solution.py:462
  (57 shorter events, 5.9 us)
Async XLA Ops:
  0.6 15.5 %copy-start.7 = (s32[512,1]{0,1:T(1,128)S(1)}, s32[512,1]{0,1:T(1,128)}, u32[]{:S(2)}) copy-start(s32[512,1]{0,1:T(1,128)} %param.15) | copy-start | bytes 6148
  4.9 11.4 %collective-permute-start = (f32[128,256]{1,0:T(8,128)}, f32[128,256]{1,0:T(8,128)S(1)}, u32[]{:S(2)}, u32[]{:S(2)}) collective-permute-start(f32[128,256]{1,0:T(8,128)} %get-tuple-element.21), channel_id=1, source_target_pairs={{64,0},{128,64},{192,128},{65,1},{129,65},{193,129},{66,2},{130,66... | collective-permute-start | bytes 393224 | tf_op jit(solution)/shard_map/ppermute | solution.py:314
  6.2 10.2 %collective-permute-start.1 = (f32[128,256]{1,0:T(8,128)}, f32[128,256]{1,0:T(8,128)S(1)}, u32[]{:S(2)}, u32[]{:S(2)}) collective-permute-start(f32[128,256]{1,0:T(8,128)} %get-tuple-element.23), channel_id=1, source_target_pairs={{0,64},{64,128},{128,192},{1,65},{65,129},{129,193},{2,66},{66,130... | collective-permute-start | bytes 393224 | tf_op jit(solution)/shard_map/ppermute | solution.py:314
  16.4 0.7 copy-start
  16.4 0.7 copy-start.1
  18.9 13.9 %collective-permute-start.4 = (f32[136,256]{1,0:T(8,128)}, f32[136,256]{1,0:T(8,128)S(1)}, u32[]{:S(2)}, u32[]{:S(2)}) collective-permute-start(f32[136,256]{1,0:T(8,128)} %close.1), channel_id=1, source_target_pairs={{0,192},{1,193},{2,194},{3,195},{4,196},{5,197},{6,198},{7,199},{8... | collective-permute-start | bytes 417800 | tf_op jit(solution)/shard_map/ppermute | solution.py:314
  21.9 10.9 %collective-permute-start.3 = (f32[136,256]{1,0:T(8,128)}, f32[136,256]{1,0:T(8,128)S(1)}, u32[]{:S(2)}, u32[]{:S(2)}) collective-permute-start(f32[136,256]{1,0:T(8,128)} %close.1), channel_id=1, source_target_pairs={{0,128},{64,192},{1,129},{65,193},{2,130},{66,194},{3,131},{67,195... | collective-permute-start | bytes 417800 | tf_op jit(solution)/shard_map/ppermute | solution.py:314
  24.5 8.3 %collective-permute-start.2 = (f32[136,256]{1,0:T(8,128)}, f32[136,256]{1,0:T(8,128)S(1)}, u32[]{:S(2)}, u32[]{:S(2)}) collective-permute-start(f32[136,256]{1,0:T(8,128)} %close.1), channel_id=1, source_target_pairs={{0,64},{64,128},{128,192},{1,65},{65,129},{129,193},{2,66},{66,130... | collective-permute-start | bytes 417800 | tf_op jit(solution)/shard_map/ppermute | solution.py:314
  32.8 0.7 copy-start.3
  32.8 0.7 copy-start.4
  32.8 0.7 copy-start.5
  40.0 12.4 %copy-start.6 = (f32[136,128]{1,0:T(8,128)S(1)}, f32[136,128]{1,0:T(8,128)}, u32[]{:S(2)}) copy-start(f32[136,128]{1,0:T(8,128)} %get-tuple-element.35) | copy-start | bytes 208900
  40.0 131.8 %all-to-all-start = ((f32[64,16,8,128]{3,2,1,0:T(8,128)}), f32[64,16,8,128]{3,2,1,0:T(8,128)}, u32[]{:S(2)}, u32[]{:S(2)}) async-start(f32[64,16,8,128]{3,2,1,0:T(8,128)} %bitcast.80), calls=%async_computation | async-start | bytes 8388608 | tf_op jit(solution)/shard_map/all_to_all | solution.py:430
  95.9 47.4 %collective-permute-start.5 = (f32[8,4,128]{2,1,0:T(4,128)S(1)}, f32[8,4,128]{2,1,0:T(4,128)S(1)}, u32[]{:S(2)}, u32[]{:S(2)}) collective-permute-start(f32[8,4,128]{2,1,0:T(4,128)S(1)} %get-tuple-element.52), channel_id=1, source_target_pairs={{0,8},{8,16},{16,24},{24,32},{32,40},{40,48},{48,56},{56,0},{1,9},... | collective-permute-start | bytes 49160 | tf_op jit(solution)/shard_map/ppermute | solution.py:321
  100.7 56.0 %collective-permute-start.11 = (f32[8,4,128]{2,1,0:T(4,128)S(1)}, f32[8,4,128]{2,1,0:T(4,128)S(1)}, u32[]{:S(2)}, u32[]{:S(2)}) collective-permute-start(f32[8,4,128]{2,1,0:T(4,128)S(1)} %get-tuple-element.46), channel_id=1, source_target_pairs={{0,56},{8,0},{16,8},{24,16},{32,24},{40,32},{48,40},{56,48},{1,57}... | collective-permute-start | bytes 49160 | tf_op jit(solution)/shard_map/ppermute | solution.py:321
  101.6 55.2 %collective-permute-start.10 = (f32[8,4,128]{2,1,0:T(4,128)S(1)}, f32[8,4,128]{2,1,0:T(4,128)S(1)}, u32[]{:S(2)}, u32[]{:S(2)}) collective-permute-start(f32[8,4,128]{2,1,0:T(4,128)S(1)} %get-tuple-element.47), channel_id=1, source_target_pairs={{0,48},{8,56},{16,0},{24,8},{32,16},{40,24},{48,32},{56,40},{1,49}... | collective-permute-start | bytes 49160 | tf_op jit(solution)/shard_map/ppermute | solution.py:321
  103.0 53.7 %collective-permute-start.9 = (f32[8,4,128]{2,1,0:T(4,128)S(1)}, f32[8,4,128]{2,1,0:T(4,128)S(1)}, u32[]{:S(2)}, u32[]{:S(2)}) collective-permute-start(f32[8,4,128]{2,1,0:T(4,128)S(1)} %get-tuple-element.48), channel_id=1, source_target_pairs={{0,40},{8,48},{16,56},{24,0},{32,8},{40,16},{48,24},{56,32},{1,41}... | collective-permute-start | bytes 49160 | tf_op jit(solution)/shard_map/ppermute | solution.py:321
  109.3 47.3 %collective-permute-start.8 = (f32[8,4,128]{2,1,0:T(4,128)S(1)}, f32[8,4,128]{2,1,0:T(4,128)S(1)}, u32[]{:S(2)}, u32[]{:S(2)}) collective-permute-start(f32[8,4,128]{2,1,0:T(4,128)S(1)} %get-tuple-element.49), channel_id=1, source_target_pairs={{0,32},{8,40},{16,48},{24,56},{32,0},{40,8},{48,16},{56,24},{1,33}... | collective-permute-start | bytes 49160 | tf_op jit(solution)/shard_map/ppermute | solution.py:321
  143.2 5.8 %collective-permute-start.6 = (f32[8,4,128]{2,1,0:T(4,128)S(1)}, f32[8,4,128]{2,1,0:T(4,128)S(1)}, u32[]{:S(2)}, u32[]{:S(2)}) collective-permute-start(f32[8,4,128]{2,1,0:T(4,128)S(1)} %get-tuple-element.51), channel_id=1, source_target_pairs={{0,16},{8,24},{16,32},{24,40},{32,48},{40,56},{48,0},{56,8},{1,17}... | collective-permute-start | bytes 49160 | tf_op jit(solution)/shard_map/ppermute | solution.py:321
  149.1 7.6 %collective-permute-start.7 = (f32[8,4,128]{2,1,0:T(4,128)S(1)}, f32[8,4,128]{2,1,0:T(4,128)S(1)}, u32[]{:S(2)}, u32[]{:S(2)}) collective-permute-start(f32[8,4,128]{2,1,0:T(4,128)S(1)} %get-tuple-element.50), channel_id=1, source_target_pairs={{0,24},{8,32},{16,40},{24,48},{32,56},{40,0},{48,8},{56,16},{1,25}... | collective-permute-start | bytes 49160 | tf_op jit(solution)/shard_map/ppermute | solution.py:321
  156.8 5.2 %collective-permute-start.12 = (f32[8,4,128]{2,1,0:T(4,128)S(1)}, f32[8,4,128]{2,1,0:T(4,128)S(1)}, u32[]{:S(2)}, u32[]{:S(2)}) collective-permute-start(f32[8,4,128]{2,1,0:T(4,128)S(1)} %get-tuple-element.45), channel_id=1, source_target_pairs={{0,1},{1,2},{2,3},{3,4},{4,5},{5,6},{6,7},{7,0},{8,9},{9,10},{10,1... | collective-permute-start | bytes 49160 | tf_op jit(solution)/shard_map/ppermute | solution.py:321
  156.8 15.0 %collective-permute-start.18 = (f32[8,4,128]{2,1,0:T(4,128)S(1)}, f32[8,4,128]{2,1,0:T(4,128)S(1)}, u32[]{:S(2)}, u32[]{:S(2)}) collective-permute-start(f32[8,4,128]{2,1,0:T(4,128)S(1)} %get-tuple-element.39), channel_id=1, source_target_pairs={{0,7},{1,0},{2,1},{3,2},{4,3},{5,4},{6,5},{7,6},{8,15},{9,8},{10,9... | collective-permute-start | bytes 49160 | tf_op jit(solution)/shard_map/ppermute | solution.py:321
  158.5 13.2 %collective-permute-start.17 = (f32[8,4,128]{2,1,0:T(4,128)S(1)}, f32[8,4,128]{2,1,0:T(4,128)S(1)}, u32[]{:S(2)}, u32[]{:S(2)}) collective-permute-start(f32[8,4,128]{2,1,0:T(4,128)S(1)} %get-tuple-element.40), channel_id=1, source_target_pairs={{0,6},{1,7},{2,0},{3,1},{4,2},{5,3},{6,4},{7,5},{8,14},{9,15},{10,... | collective-permute-start | bytes 49160 | tf_op jit(solution)/shard_map/ppermute | solution.py:321
  161.6 10.2 %collective-permute-start.16 = (f32[8,4,128]{2,1,0:T(4,128)S(1)}, f32[8,4,128]{2,1,0:T(4,128)S(1)}, u32[]{:S(2)}, u32[]{:S(2)}) collective-permute-start(f32[8,4,128]{2,1,0:T(4,128)S(1)} %get-tuple-element.41), channel_id=1, source_target_pairs={{0,5},{1,6},{2,7},{3,0},{4,1},{5,2},{6,3},{7,4},{8,13},{9,14},{10,... | collective-permute-start | bytes 49160 | tf_op jit(solution)/shard_map/ppermute | solution.py:321
  161.6 10.2 %collective-permute-start.15 = (f32[8,4,128]{2,1,0:T(4,128)S(1)}, f32[8,4,128]{2,1,0:T(4,128)S(1)}, u32[]{:S(2)}, u32[]{:S(2)}) collective-permute-start(f32[8,4,128]{2,1,0:T(4,128)S(1)} %get-tuple-element.42), channel_id=1, source_target_pairs={{0,4},{1,5},{2,6},{3,7},{4,0},{5,1},{6,2},{7,3},{8,12},{9,13},{10,... | collective-permute-start | bytes 49160 | tf_op jit(solution)/shard_map/ppermute | solution.py:321
  162.0 5.0 %collective-permute-start.13 = (f32[8,4,128]{2,1,0:T(4,128)S(1)}, f32[8,4,128]{2,1,0:T(4,128)S(1)}, u32[]{:S(2)}, u32[]{:S(2)}) collective-permute-start(f32[8,4,128]{2,1,0:T(4,128)S(1)} %get-tuple-element.44), channel_id=1, source_target_pairs={{0,2},{1,3},{2,4},{3,5},{4,6},{5,7},{6,0},{7,1},{8,10},{9,11},{10,... | collective-permute-start | bytes 49160 | tf_op jit(solution)/shard_map/ppermute | solution.py:321
  167.1 4.7 %collective-permute-start.14 = (f32[8,4,128]{2,1,0:T(4,128)S(1)}, f32[8,4,128]{2,1,0:T(4,128)S(1)}, u32[]{:S(2)}, u32[]{:S(2)}) collective-permute-start(f32[8,4,128]{2,1,0:T(4,128)S(1)} %get-tuple-element.43), channel_id=1, source_target_pairs={{0,3},{1,4},{2,5},{3,6},{4,7},{5,0},{6,1},{7,2},{8,11},{9,12},{10,... | collective-permute-start | bytes 49160 | tf_op jit(solution)/shard_map/ppermute | solution.py:321
  171.8 0.7 copy-start.2

commit v4 on v2

--- a/solution.py
+++ b/solution.py
@@ -20,7 +20,7 @@
     return pl.CostEstimate(flops=flops, bytes_accessed=moved, transcendentals=0)
 
 
-def params(mib=16):
+def params(mib=48):
     return pltpu.CompilerParams(vmem_limit_bytes=mib << 20)
 
 
@@ -31,22 +31,31 @@
     return after / total, own / total, 0.5 * own, 0.5 * after
 
 
-def head_kernel(rank_ref, f_ref, h_ref, x_ref, first_ref, last_ref, out_ref):
-    rows_of = weights_x(rank_ref, h_ref)
-    weight = lambda i, k: rows_of[i][0:1, (2 * k) % 128 : (2 * k) % 128 + 1]
-    far_before = jnp.where(rank_ref[0] > 0, weight(3, -1), 0.0)
-    before = -f_ref[15, 0] * far_before * weight(1, -1)
-    total = None
-    for j in range(16):
-        v = f_ref[15, j] * weight(2, j)
-        if j < 15:
-            v = v + f_ref[15, j + 1] * weight(3, j)
-        term = (before - v * weight(0, j)) * x_ref[2 * j] + v * x_ref[2 * j + 1]
-        total = term if total is None else total + term
-        before = -v * weight(1, j)
-    out_ref[...] = total
-    first_ref[...] = x_ref[0]
-    last_ref[...] = x_ref[31] - weight(0, 15) * x_ref[30]
+def head_kernel(rank_ref, f_ref, h_ref, x_ref, first_ref, last_ref, out_ref, w_ref):
+    @pl.when(pl.program_id(0) == 0)
+    def _():
+        rows_of = weights_x(rank_ref, h_ref)
+        weight = lambda i, k: jnp.broadcast_to(rows_of[i][:, (2 * k) % 128 : (2 * k) % 128 + 1], (8, 128))
+        far_before = jnp.where(rank_ref[0] > 0, weight(3, -1), 0.0)
+        before = -f_ref[15, 0] * far_before * weight(1, -1)
+        for j in range(16):
+            v = f_ref[15, j] * weight(2, j)
+            if j < 15:
+                v = v + f_ref[15, j + 1] * weight(3, j)
+            w_ref[2 * j] = before - v * weight(0, j)
+            w_ref[2 * j + 1] = v
+            before = -v * weight(1, j)
+        w_ref[32] = weight(0, 15)
+
+    for r in range(x_ref.shape[1] // 8):
+        for half in range(2):
+            at = (slice(8 * r, 8 * r + 8), slice(128 * half, 128 * half + 128))
+            total = w_ref[0] * x_ref[(0, *at)]
+            for x in range(1, 32):
+                total = total + w_ref[x] * x_ref[(x, *at)]
+            out_ref[at] = total
+            first_ref[at] = x_ref[(0, *at)]
+            last_ref[at] = x_ref[(31, *at)] - w_ref[32] * x_ref[(30, *at)]
 
 
 def close_kernel(g_ref, row_ref, own_ref, right_ref, left_ref, out_ref):
@@ -87,10 +96,7 @@
     return detail, chosen[:, 0:half] + dot_nt(load[:, 0:half], factor), near, b
 
 
-def table_kernel(
-    rank_ref, rank_x_ref, h_ref, even_ref, odd_ref, f_ref, g_ref, hx_ref, fx_ref,
-    high_ref, low_ref, row_ref, x_high_ref, x_low_ref, x_row_ref,
-):
+def table_kernel(rank_ref, h_ref, even_ref, odd_ref, f_ref, g_ref, high_ref, low_ref, row_ref):
     at = jnp.maximum(rank_ref[0] * 256 - 2, 0)
     one = lambda value: jnp.full((1, 1), value, F32)
     h_even, h_odd = one(h_ref[at]), one(h_ref[at + 1])
@@ -119,6 +125,8 @@
     row_ref[6:7] = jnp.broadcast_to(gain[:, 127:128], (1, 128))
     row_ref[7:8] = jnp.zeros((1, 128), F32)
 
+
+def table_x_kernel(rank_x_ref, hx_ref, fx_ref, x_high_ref, x_low_ref, x_row_ref):
     base = rank_x_ref[0] * 32
     node = lax.broadcasted_iota(jnp.int32, (128, 128), 0)
     place = lax.broadcasted_iota(jnp.int32, (128, 128), 1)
@@ -156,10 +164,25 @@
 
 
 def main_kernel(
-    x_row_ref, x_ref, right_ref, left_ref, x_high_ref, x_low_ref, high_ref, low_ref,
-    dz_ref, cz_ref, column_ref, v_ref,
+    rank_x_ref, h_ref, x_row_ref, x_ref, right_ref, left_ref, x_high_ref, x_low_ref, high_ref, low_ref,
+    detail_x_ref, dz_ref, cz_ref, column_ref, v_ref, w_ref,
 ):
+    @pl.when(pl.program_id(0) == 0)
+    def _():
+        rows_of = weights_x(rank_x_ref, h_ref)
+        for j in range(16):
+            for i in range(2):
+                w_ref[i, j] = jnp.broadcast_to(rows_of[i][:, 2 * j : 2 * j + 1], (8, 128))
+
     chunk = x_ref.shape[1]
+    for r in range(chunk // 8):
+        for half in range(2):
+            at = (slice(8 * r, 8 * r + 8), slice(128 * half, 128 * half + 128))
+            for j in range(16):
+                after = x_ref[(2 * j + 2, *at)] if j < 15 else right_ref[at]
+                detail_x_ref[(j, *at)] = (
+                    x_ref[(2 * j + 1, *at)] - w_ref[0, j] * x_ref[(2 * j, *at)] - w_ref[1, j] * after
+                )
     for step in range(chunk // 8):
         rows = slice(step * 8, step * 8 + 8)
         nodes = x_ref[:, rows, :].reshape(256, 256)
@@ -186,24 +209,6 @@
     column_ref[...] = message
 
 
-def output_kernel(
-    rank_ref, rank_x_ref, g_ref, h_ref, x_ref, right_ref, dz_ref, plane_ref, all_ref, row_ref,
-    detail_x_ref, detail_z_ref,
-):
-    rows_of = weights_x(rank_x_ref, h_ref)
-    weight = lambda i, k: rows_of[i][0:1, 2 * k : 2 * k + 1]
-    for j in range(16):
-        after = x_ref[2 * j + 2] if j < 15 else right_ref[...]
-        detail_x_ref[j] = x_ref[2 * j + 1] - weight(0, j) * x_ref[2 * j] - weight(1, j) * after
-    rank = rank_ref[0]
-    chunk = x_ref.shape[1]
-    rows = pl.ds(pl.multiple_of(pl.program_id(0) * chunk, chunk), chunk)
-    edge = jnp.where(rank < 7, all_ref[jnp.minimum(rank + 1, 7), rows, :], 0.0)
-    for k in range(16):
-        spread = jnp.broadcast_to(edge[:, k : k + 1], (chunk, 128))
-        detail_z_ref[k] = dz_ref[k] + g_ref[k] * plane_ref[:, 0:128] + spread * row_ref[0:1, :]
-
-
 def carry_kernel(g_ref, one_ref, two_ref, three_ref, high_ref, low_ref, row_ref, column_ref, plane_ref, out_ref):
     carry = two_ref[0:128, :] + two_ref[128:129, :] * three_ref[0:128, :]
     carry = one_ref[0:128, :] + one_ref[128:129, :] * carry
@@ -227,7 +232,7 @@
 
 
 def last_kernel(
-    rank_ref, g_ref, place_ref, dz_ref, cz_ref, plane_ref, all_ref, row_ref, out_ref
+    rank_ref, g_ref, place_ref, dz_ref, cz_ref, plane_ref, all_ref, row_ref, detail_ref, out_ref
 ):
     rank = rank_ref[0]
 
@@ -254,6 +259,7 @@
         detail = dz_ref[k] + g * plane_ref[:, 0:128] + right_k * d_right
         coarse = cz_ref[k] + g * plane_ref[:, 128:256] + right_k * c_right
         coarse = coarse + spread(left, k) * c_left + spread(carry, k) * gain
+        detail_ref[k] = detail
         for i in range(16):
             c8, d8 = coarse[8 * i : 8 * i + 8], detail[8 * i : 8 * i + 8]
             block = 32 * k + 2 * i
@@ -288,6 +294,7 @@
         in_specs=[s, s, whole((1, 128)), nodes],
         out_specs=[thin, thin, thin],
         out_shape=[plane, plane, plane],
+        scratch_shapes=[VMEM((33, 8, 128), F32)],
         cost_estimate=cost(64 * 32768, 4 << 20),
         name="head",
     )(rank_x, operator_x, space_x, nodal_field)
@@ -297,21 +304,15 @@
     near_space = lax.dynamic_slice_in_dim(spacing_z, rank_z[0] * 256, 256)
     square = jax.ShapeDtypeStruct((256, 256), BF16)
     oblong = jax.ShapeDtypeStruct((128, 256), BF16)
-    high, low, rows, x_high, x_low, x_rows = pl.pallas_call(
-        table_kernel,
-        in_specs=[s, s, s, v, v, v, v, v, v],
-        out_specs=[v] * 6,
-        out_shape=[
-            square, square, jax.ShapeDtypeStruct((8, 128), F32),
-            oblong, oblong, jax.ShapeDtypeStruct((32, 128), F32),
-        ],
+    x_high, x_low, x_rows = pl.pallas_call(
+        table_x_kernel,
+        in_specs=[s, v, v],
+        out_specs=[v] * 3,
+        out_shape=[oblong, oblong, jax.ShapeDtypeStruct((32, 128), F32)],
         compiler_params=params(),
-        cost_estimate=cost(12 * 256 * 256 * 128, 1 << 20),
-        name="table",
-    )(
-        rank_z, rank_x, spacing_z, near_space[0::2].reshape(1, 128), near_space[1::2].reshape(1, 128),
-        operator_z, persist_z.reshape(1, 128), space_x, operator_x,
-    )
+        cost_estimate=cost(1 << 22, 1 << 17),
+        name="table_x",
+    )(rank_x, space_x, operator_x)
 
     ended = pl.pallas_call(
         close_kernel,
@@ -322,24 +323,41 @@
     )(persist_x, x_rows, own, right, left)
     one, two, three = (shift(ended, "gx", by) for by in (1, 2, 3))
 
-    dz, cz, columns = pl.pallas_call(
+    high, low, rows = pl.pallas_call(
+        table_kernel,
+        in_specs=[s, s, v, v, v, v],
+        out_specs=[v] * 3,
+        out_shape=[square, square, jax.ShapeDtypeStruct((8, 128), F32)],
+        compiler_params=params(),
+        cost_estimate=cost(12 * 256 * 256 * 128, 1 << 20),
+        name="table",
+    )(
+        rank_z, spacing_z, near_space[0::2].reshape(1, 128), near_space[1::2].reshape(1, 128),
+        operator_z, persist_z.reshape(1, 128),
+    )
+
+    detail_x, dz, cz, columns = pl.pallas_call(
         main_kernel,
         grid=grid,
         in_specs=[
-            whole((32, 128)), nodes, thin, thin,
+            s, whole((1, 128)), whole((32, 128)), nodes, thin, thin,
             whole((128, 256)), whole((128, 256)), whole((256, 256)), whole((256, 256)),
         ],
-        out_specs=[third, third, pl.BlockSpec((chunk, 128), lambda i: (i, 0))],
+        out_specs=[
+            pl.BlockSpec((16, chunk, 256), lambda i: (0, i, 0)),
+            third, third, pl.BlockSpec((chunk, 128), lambda i: (i, 0)),
+        ],
         out_shape=[
+            jax.ShapeDtypeStruct((16, 128, 256), F32),
             jax.ShapeDtypeStruct((16, 128, 128), F32),
             jax.ShapeDtypeStruct((16, 128, 128), F32),
             jax.ShapeDtypeStruct((128, 128), F32),
         ],
-        scratch_shapes=[VMEM((16, chunk, 256), F32)],
+        scratch_shapes=[VMEM((16, chunk, 256), F32), VMEM((2, 16, 8, 128), F32)],
         compiler_params=params(),
         cost_estimate=cost(6 * 2048 * 256 * 256, 10 << 20),
         name="main",
-    )(x_rows, nodal_field, right, left, x_high, x_low, high, low)
+    )(rank_x, space_x, x_rows, nodal_field, right, left, x_high, x_low, high, low)
 
     plane_pass, message = pl.pallas_call(
         carry_kernel,
@@ -358,32 +376,20 @@
     earlier = (targets[None, :] == targets[:, None]) & (positions[None, :] < positions[:, None])
     placed = targets * capacity + jnp.sum(earlier.astype(jnp.int32), axis=1)
 
-    outgoing = pl.pallas_call(
+    detail_z, outgoing = pl.pallas_call(
         last_kernel,
         in_specs=[s, s, s, v, v, v, v, v],
-        out_specs=v,
-        out_shape=jax.ShapeDtypeStruct((group * capacity, 8, 128), F32),
+        out_specs=[v, v],
+        out_shape=[
+            jax.ShapeDtypeStruct((16, 128, 128), F32),
+            jax.ShapeDtypeStruct((group * capacity, 8, 128), F32),
+        ],
         compiler_params=params(),
         name="last",
     )(rank_z, persist_x, placed, dz, cz, plane_pass, gathered, rows)
     incoming = lax.all_to_all(
         outgoing.reshape(group, capacity, 8, 128), ("gy", "gz"), split_axis=0, concat_axis=0, tiled=True
     )
-    detail_x, detail_z = pl.pallas_call(
-        output_kernel,
-        grid=grid,
-        in_specs=[
-            s, s, s, whole((1, 128)), nodes, thin, third, thin, whole((8, 128, 128)), whole((8, 128)),
-        ],
-        out_specs=[pl.BlockSpec((16, chunk, 256), lambda i: (0, i, 0)), third],
-        out_shape=[
-            jax.ShapeDtypeStruct((16, 128, 256), F32),
-            jax.ShapeDtypeStruct((16, 128, 128), F32),
-        ],
-        compiler_params=params(),
-        cost_estimate=cost(1 << 20, 8 << 20),
-        name="output",
-    )(rank_z, rank_x, persist_x, space_x, nodal_field, right, dz, plane_pass, gathered, rows)
     received = incoming.reshape(1, group, capacity, 2, LINES, 128)
     return (detail_x, detail_z, received)
 

time: 168 us -> 166 us (0.988)
  blocking collectives: 13.3 us -> 121 us
  waiting for transfers between devices: 90.4 us -> 0.78 us
  starting transfers between devices: 27.5 us -> 15.7 us
  local copies, waits for them, and re-layouts: 16.2 us -> 6.33 us
    all_to_all x0 -> x1, blocking collectives: none -> 108 us  [local(): lax.all_to_all(outgoing.reshape(group, capacity, 8, 128), ('gy', 'gz'), s...]
    all_to_all x1 -> x0, waiting for transfers between devices: 90.4 us -> none  [local(): lax.all_to_all(outgoing.reshape(group, capacity, 8, 128), ('gy', 'gz'), s...]
    all_to_all x1 -> x0, starting transfers between devices: 12 us -> none  [local(): lax.all_to_all(outgoing.reshape(group, capacity, 8, 128), ('gy', 'gz'), s...]
    unnamed x35 -> x27, local copies, waits for them, and re-layouts: 15.7 us -> 5.81 us
    pallas_call x1, Pallas kernels: 2.2 us -> 4.58 us  [local(): pl.pallas_call(last_kernel, in_specs=[s, s, s, v, v, v, v, v], out_specs=...]
  transfers between devices with their start and end apart: 6 -> 5, of which waited for: 1 -> 1; matrix products, arithmetic and copies ran while one was open for 0% -> 0% of each run, Pallas kernels for 6% -> 5%
where the time goes in v4:
time: 166 us
  blocking collectives  121 us (73%)
  Pallas kernels  20.6 us (12%)
  starting transfers between devices  15.7 us (9%)
  local copies, waits for them, and re-layouts  6.33 us (4%)
    all_to_all x1, blocking collectives, local(): lax.all_to_all(outgoing.reshape(group, capacity, 8, 128), ('gy', 'gz'), s...  108 us
    ppermute x5, starting transfers between devices, shift(): lax.ppermute(value, axis, [(i, i + by) for i in range(count) if 0 <= i +...  15.7 us
    all_gather x1, blocking collectives, local(): gathered = lax.all_gather(message, 'gz')  13.3 us
    pallas_call x1, Pallas kernels, local(): pl.pallas_call(main_kernel, grid=grid, in_specs=[s, whole((1, 128)), whol...  6.82 us
    unnamed x27, local copies, waits for them, and re-layouts  5.81 us
    pallas_call x1, Pallas kernels, local(): pl.pallas_call(last_kernel, in_specs=[s, s, s, v, v, v, v, v], out_specs=...  4.58 us
    pallas_call x1, Pallas kernels, local(): pl.pallas_call(head_kernel, grid=grid, in_specs=[s, s, whole((1, 128)), n...  4.32 us
  transfers between devices with their start and end apart: 5, of which 1 were waited for; matrix products, arithmetic and copies ran while one was open for 0% of the time, Pallas kernels for 5%

profile of v4, /device:TPU:8, one launch (start us, length us, event | category | flops | bytes accessed | tf_op | source)
XLA Modules:
  0.0 165.8 jit_solution(1337097179092650454)
XLA Ops:
  0.7 0.0 copy-start.7
  0.7 4.3 %head.1 = (f32[128,256]{1,0:T(8,128)}, f32[128,256]{1,0:T(8,128)}, f32[128,256]{1,0:T(8,128)}) custom-call(s32[1]{0:T(128)} %bitcast.rank_x_ref.rank_ref, f32[16,16]{1,0:T(8,128)} %f_ref.2, f32[1,128]{1,0:T(1,128)} %bitcast.11, f32[32,128,256]{2,1,0:T(8,128)} %x_ref.3), custom_call_target="tpu_custom_call" | custom-call | flops 2097152 | bytes 4194304 | tf_op jit(solution)/shard_map/head/pallas_call | solution.py:291
  5.0 1.3 collective-permute-start
  6.3 4.6 %collective-permute-start.1 = (f32[128,256]{1,0:T(8,128)}, f32[128,256]{1,0:T(8,128)S(1)}, u32[]{:S(2)}, u32[]{:S(2)}) collective-permute-start(f32[128,256]{1,0:T(8,128)} %get-tuple-element.22), channel_id=1, source_target_pairs={{0,64},{64,128},{128,192},{1,65},{65,129},{129,193},{2,66},{66,130... | collective-permute-start | bytes 393224 | tf_op jit(solution)/shard_map/ppermute | solution.py:272
  10.9 0.0 copy-done.6
  10.9 0.0 copy-done.8
  10.9 1.1 table_x.1
  12.1 0.6 copy-done.4
  12.6 0.2 convert_reduce_fusion
  12.9 0.0 collective-permute-done.right_ref
  12.9 0.8 collective-permute-done.1.left_ref
  13.7 0.7 copy-done.2
  14.3 1.8 %close.1 = f32[136,256]{1,0:T(8,128)} custom-call(f32[16]{0:T(128)} %g_ref.5, f32[32,128]{1,0:T(8,128)} %copy-done.4, f32[128,256]{1,0:T(8,128)} %get-tuple-element.30.own_ref, f32[128,256]{1,0:T(8,128)} %copy-done, f32[128,256]{1,0:T(8,128)} %copy-done.2), custom_call_target="tpu_custom_call" | custom-call | tf_op jit(solution)/shard_map/close/pallas_call | solution.py:317
  16.1 5.8 %collective-permute-start.4 = (f32[136,256]{1,0:T(8,128)}, f32[136,256]{1,0:T(8,128)S(1)}, u32[]{:S(2)}, u32[]{:S(2)}) collective-permute-start(f32[136,256]{1,0:T(8,128)} %close.1), channel_id=1, source_target_pairs={{0,192},{1,193},{2,194},{3,195},{4,196},{5,197},{6,198},{7,199},{8... | collective-permute-start | bytes 417800 | tf_op jit(solution)/shard_map/ppermute | solution.py:272
  21.9 1.3 collective-permute-start.3
  23.2 2.8 %collective-permute-start.2 = (f32[136,256]{1,0:T(8,128)}, f32[136,256]{1,0:T(8,128)S(1)}, u32[]{:S(2)}, u32[]{:S(2)}) collective-permute-start(f32[136,256]{1,0:T(8,128)} %close.1), channel_id=1, source_target_pairs={{0,64},{64,128},{128,192},{1,65},{65,129},{129,193},{2,66},{66,130... | collective-permute-start | bytes 417800 | tf_op jit(solution)/shard_map/ppermute | solution.py:272
  26.0 0.1 dynamic_slice.3
  26.1 0.2 slice.7
  26.3 0.2 slice.6
  26.6 1.1 table.1
  27.7 0.9 copy-done.1
  28.6 0.9 copy-done.3
  29.5 0.7 copy-done.5
  30.2 6.8 %main.1 = (f32[16,128,256]{2,1,0:T(8,128)}, f32[16,128,128]{2,1,0:T(8,128)S(1)}, f32[16,128,128]{2,1,0:T(8,128)S(1)}, f32[128,128]{1,0:T(8,128)S(1)}) custom-call(s32[1]{0:T(128)} %bitcast.rank_x_ref.rank_ref, f32[1,128]{1,0:T(1,128)S(1)} %bitcast.13, f32[32,128]{1,0:T(8,128)S(1)} %copy-done.5, f32[32,128,256]{2,1,0:T(8,128)} %x_ref.3, ...), custom_call_target="tpu_custom_call" | custom-call | flops 805306368 | bytes 10485760 | tf_op jit(solution)/shard_map/main/pallas_call | solution.py:339
  37.1 0.0 collective-permute-done.4.three_ref
  37.1 0.0 collective-permute-done.3.two_ref
  37.1 0.0 collective-permute-done.2.one_ref
  37.1 0.9 carry.1
  37.9 13.3 %all-gather = f32[1024,128]{1,0:T(8,128)S(1)} all-gather(f32[128,128]{1,0:T(8,128)S(1)} %get-tuple-element.34), channel_id=2, replica_groups=mesh['gx'=4,'gy'=8,'gz'=8] {'gz'}, dimensions={0}, use_global_device_ids=true | all-gather | bytes 589824 | tf_op jit(solution)/shard_map/all_gather | solution.py:370
  51.3 4.6 %last.1 = (f32[16,128,128]{2,1,0:T(8,128)}, f32[1024,8,128]{2,1,0:T(8,128)}) custom-call(s32[1]{0:T(128)} %bitcast.2.rank_ref, f32[16]{0:T(128)S(1)} %copy-done.7, s32[512]{0:T(512)S(1)} %multiply_add_fusion.place_ref, f32[16,128,128]{2,1,0:T(8,128)S(1)} %get-tuple-element.28.dz_ref, f32[16,128,128]{2,1,0:T(8,128)S(1)} %get-tuple-element.29.cz_ref, ...), custom_call_target="tpu_custom_call" | custom-call | tf_op jit(solution)/shard_map/last/pallas_call | solution.py:379
  55.9 107.9 %all_to_all.5 = f32[64,16,8,128]{3,2,1,0:T(8,128)S(1)} all-to-all(f32[64,16,8,128]{3,2,1,0:T(8,128)} %bitcast.18), channel_id=1, replica_groups=mesh['gx'=4,'gy'=8,'gz'=8] {'gy','gz'}, dimensions={0} | all-to-all | bytes 8388608 | tf_op jit(solution)/shard_map/all_to_all | solution.py:390
  163.7 2.0 %copy.12 = f32[1,64,16,2,4,128]{5,4,3,2,1,0:T(4,128)} copy(f32[1,64,16,2,4,128]{5,4,3,2,1,0:T(4,128)S(1)} %bitcast.17) | data formatting | bytes 8388608
  (19 shorter events, 0.0 us)
Async XLA Ops:
  0.6 10.2 %copy-start.6 = (f32[16,16]{1,0:T(8,128)S(1)}, f32[16,16]{1,0:T(8,128)}, u32[]{:S(2)}) copy-start(f32[16,16]{1,0:T(8,128)} %f_ref.2) | copy-start | bytes 3076
  0.6 10.2 %copy-start.8 = (f32[128]{0:T(128)S(1)}, f32[128]{0:T(128)}, u32[]{:S(2)}) copy-start(f32[128]{0:T(128)} %param.9) | copy-start | bytes 1540
  0.7 12.0 %copy-start.12 = (s32[512,1]{0,1:T(1,128)S(1)}, s32[512,1]{0,1:T(1,128)}, u32[]{:S(2)}) copy-start(s32[512,1]{0,1:T(1,128)} %param.15) | copy-start | bytes 6148
  0.7 25.4 %copy-start.9 = (f32[2048]{0:T(1024)S(1)}, f32[2048]{0:T(1024)}, u32[]{:S(2)}) copy-start(f32[2048]{0:T(1024)} %h_ref.1) | copy-start | bytes 24580
  0.7 25.9 %copy-start.11 = (f32[128]{0:T(128)S(1)}, f32[128]{0:T(128)}, u32[]{:S(2)}) copy-start(f32[128]{0:T(128)} %param.14) | copy-start | bytes 1540
  0.7 25.9 %copy-start.10 = (f32[128,128]{1,0:T(8,128)S(1)}, f32[128,128]{1,0:T(8,128)}, u32[]{:S(2)}) copy-start(f32[128,128]{1,0:T(8,128)} %f_ref.3) | copy-start | bytes 196612
  0.7 36.4 %copy-start.7 = (f32[16]{0:T(128)S(1)}, f32[16]{0:T(128)}, u32[]{:S(2)}) copy-start(f32[16]{0:T(128)} %g_ref.5) | copy-start | bytes 196
  5.0 7.9 %collective-permute-start = (f32[128,256]{1,0:T(8,128)}, f32[128,256]{1,0:T(8,128)S(1)}, u32[]{:S(2)}, u32[]{:S(2)}) collective-permute-start(f32[128,256]{1,0:T(8,128)} %get-tuple-element.21), channel_id=1, source_target_pairs={{64,0},{128,64},{192,128},{65,1},{129,65},{193,129},{66,2},{130,66... | collective-permute-start | bytes 393224 | tf_op jit(solution)/shard_map/ppermute | solution.py:272
  6.3 7.4 %collective-permute-start.1 = (f32[128,256]{1,0:T(8,128)}, f32[128,256]{1,0:T(8,128)S(1)}, u32[]{:S(2)}, u32[]{:S(2)}) collective-permute-start(f32[128,256]{1,0:T(8,128)} %get-tuple-element.22), channel_id=1, source_target_pairs={{0,64},{64,128},{128,192},{1,65},{65,129},{129,193},{2,66},{66,130... | collective-permute-start | bytes 393224 | tf_op jit(solution)/shard_map/ppermute | solution.py:272
  12.0 0.6 copy-start.4
  12.9 0.8 copy-start
  13.7 0.7 copy-start.2
  16.1 20.9 %collective-permute-start.4 = (f32[136,256]{1,0:T(8,128)}, f32[136,256]{1,0:T(8,128)S(1)}, u32[]{:S(2)}, u32[]{:S(2)}) collective-permute-start(f32[136,256]{1,0:T(8,128)} %close.1), channel_id=1, source_target_pairs={{0,192},{1,193},{2,194},{3,195},{4,196},{5,197},{6,198},{7,199},{8... | collective-permute-start | bytes 417800 | tf_op jit(solution)/shard_map/ppermute | solution.py:272
  21.9 15.1 %collective-permute-start.3 = (f32[136,256]{1,0:T(8,128)}, f32[136,256]{1,0:T(8,128)S(1)}, u32[]{:S(2)}, u32[]{:S(2)}) collective-permute-start(f32[136,256]{1,0:T(8,128)} %close.1), channel_id=1, source_target_pairs={{0,128},{64,192},{1,129},{65,193},{2,130},{66,194},{3,131},{67,195... | collective-permute-start | bytes 417800 | tf_op jit(solution)/shard_map/ppermute | solution.py:272
  23.2 13.8 %collective-permute-start.2 = (f32[136,256]{1,0:T(8,128)}, f32[136,256]{1,0:T(8,128)S(1)}, u32[]{:S(2)}, u32[]{:S(2)}) collective-permute-start(f32[136,256]{1,0:T(8,128)} %close.1), channel_id=1, source_target_pairs={{0,64},{64,128},{128,192},{1,65},{65,129},{129,193},{2,66},{66,130... | collective-permute-start | bytes 417800 | tf_op jit(solution)/shard_map/ppermute | solution.py:272
  27.7 0.9 copy-start.1
  28.6 0.9 copy-start.3
  29.5 0.7 copy-start.5

commit v5 on v4

--- a/solution.py
+++ b/solution.py
@@ -56,12 +56,6 @@
             out_ref[at] = total
             first_ref[at] = x_ref[(0, *at)]
             last_ref[at] = x_ref[(31, *at)] - w_ref[32] * x_ref[(30, *at)]
-
-
-def close_kernel(g_ref, row_ref, own_ref, right_ref, left_ref, out_ref):
-    total = own_ref[...] + row_ref[15:16, 0:1] * right_ref[...] + row_ref[31:32, 0:1] * left_ref[...]
-    out_ref[0:128, :] = total
-    out_ref[128:136, :] = jnp.full((8, 256), g_ref[15], F32)
 
 
 def split(value):
@@ -314,13 +308,8 @@
         name="table_x",
     )(rank_x, space_x, operator_x)
 
-    ended = pl.pallas_call(
-        close_kernel,
-        in_specs=[s, v, v, v, v],
-        out_specs=v,
-        out_shape=jax.ShapeDtypeStruct((136, 256), F32),
-        name="close",
-    )(persist_x, x_rows, own, right, left)
+    total = own + x_rows[15:16, 0:1] * right + x_rows[31:32, 0:1] * left
+    ended = jnp.concatenate([total, jnp.broadcast_to(persist_x[15], (8, 256))], axis=0)
     one, two, three = (shift(ended, "gx", by) for by in (1, 2, 3))
 
     high, low, rows = pl.pallas_call(

time: 166 us -> 164 us (0.988)
  other arithmetic: 0.25 us -> 2.56 us
  local copies, waits for them, and re-layouts: 6.33 us -> 4.27 us
  Pallas kernels: 20.6 us -> 18.8 us
    unnamed x27 -> x15, local copies, waits for them, and re-layouts: 5.81 us -> 2.04 us
    add x0 -> x1, other arithmetic: none -> 2.31 us  [local(): total = own + x_rows[15:16, 0:1] * right + x_rows[31:32, 0:1] * left]
    pallas_call x1 -> x0, Pallas kernels: 1.78 us -> none  [local(): pl.pallas_call(close_kernel, in_specs=[s, v, v, v, v], out_specs=v, out_s...]
  transfers between devices with their start and end apart: 5 -> 5, of which waited for: 1 -> 1; matrix products, arithmetic and copies ran while one was open for 0% -> 1% of each run, Pallas kernels for 5% -> 6%
where the time goes in v5:
time: 164 us
  blocking collectives  121 us (74%)
  Pallas kernels  18.8 us (11%)
  starting transfers between devices  15.7 us (10%)
  local copies, waits for them, and re-layouts  4.27 us (3%)
  other arithmetic  2.56 us (2%)
    all_to_all x1, blocking collectives, local(): lax.all_to_all(outgoing.reshape(group, capacity, 8, 128), ('gy', 'gz'), s...  108 us
    ppermute x5, starting transfers between devices, shift(): lax.ppermute(value, axis, [(i, i + by) for i in range(count) if 0 <= i +...  15.7 us
    all_gather x1, blocking collectives, local(): gathered = lax.all_gather(message, 'gz')  13.3 us
    pallas_call x1, Pallas kernels, local(): pl.pallas_call(main_kernel, grid=grid, in_specs=[s, whole((1, 128)), whol...  6.82 us
    pallas_call x1, Pallas kernels, local(): pl.pallas_call(last_kernel, in_specs=[s, s, s, v, v, v, v, v], out_specs=...  4.55 us
    pallas_call x1, Pallas kernels, local(): pl.pallas_call(head_kernel, grid=grid, in_specs=[s, s, whole((1, 128)), n...  4.32 us
  transfers between devices with their start and end apart: 5, of which 1 were waited for; matrix products, arithmetic and copies ran while one was open for 1% of the time, Pallas kernels for 6%

profile of v5, /device:TPU:8, one launch (start us, length us, event | category | flops | bytes accessed | tf_op | source)
XLA Modules:
  0.0 163.7 jit_solution(8977245099767031972)
XLA Ops:
  0.6 0.0 copy-start
  0.6 0.0 copy-start.2
  0.7 0.0 copy-start.1
  0.7 4.3 %head.1 = (f32[128,256]{1,0:T(8,128)}, f32[128,256]{1,0:T(8,128)}, f32[128,256]{1,0:T(8,128)}) custom-call(s32[1]{0:T(128)} %bitcast.rank_x_ref.rank_ref, f32[16,16]{1,0:T(8,128)} %f_ref.2, f32[1,128]{1,0:T(1,128)} %bitcast.14, f32[32,128,256]{2,1,0:T(8,128)} %x_ref.3), custom_call_target="tpu_custom_call" | custom-call | flops 2097152 | bytes 4194304 | tf_op jit(solution)/shard_map/head/pallas_call | solution.py:285
  5.0 1.3 collective-permute-start
  6.3 4.6 %collective-permute-start.1 = (f32[128,256]{1,0:T(8,128)}, f32[128,256]{1,0:T(8,128)S(1)}, u32[]{:S(2)}, u32[]{:S(2)}) collective-permute-start(f32[128,256]{1,0:T(8,128)} %get-tuple-element.22), channel_id=1, source_target_pairs={{0,64},{64,128},{128,192},{1,65},{65,129},{129,193},{2,66},{66,130... | collective-permute-start | bytes 393224 | tf_op jit(solution)/shard_map/ppermute | solution.py:266
  10.9 1.1 table_x.1
  12.0 0.0 copy-done.1
  12.1 0.6 slice.19
  12.6 0.6 fusion.1
  13.2 0.2 convert_reduce_fusion
  13.5 0.0 collective-permute-done.right_ref
  13.5 0.2 collective-permute-done.1.left_ref
  13.7 2.3 %multiply_add_fusion = f32[128,256]{1,0:T(8,128)S(1)} fusion(f32[128,256]{1,0:T(8,128)S(1)} %collective-permute-done.1.left_ref, f32[128,256]{1,0:T(8,128)} %get-tuple-element.30, f32[128,256]{1,0:T(8,128)S(1)} %collective-permute-done.right_ref, f32[]{:T(128)} %bitcast.8, f32[]{:T(128)} %bitcast.7), kind=kLoop, calls=%fused_computation.3 | loop fusion | flops 131072 | bytes 524296 | tf_op jit(solution)/shard_map/add | solution.py:311
  16.0 0.6 concatenate.3
  16.6 5.8 %collective-permute-start.4 = (f32[136,256]{1,0:T(8,128)S(1)}, f32[136,256]{1,0:T(8,128)S(1)}, u32[]{:S(2)}, u32[]{:S(2)}) collective-permute-start(f32[136,256]{1,0:T(8,128)S(1)} %concatenate.3), channel_id=1, source_target_pairs={{0,192},{1,193},{2,194},{3,195},{4,196},{5,197},{6,198},{7,199},{8... | collective-permute-start | bytes 417800 | tf_op jit(solution)/shard_map/ppermute | solution.py:266
  22.4 1.3 collective-permute-start.3
  23.7 2.8 %collective-permute-start.2 = (f32[136,256]{1,0:T(8,128)S(1)}, f32[136,256]{1,0:T(8,128)S(1)}, u32[]{:S(2)}, u32[]{:S(2)}) collective-permute-start(f32[136,256]{1,0:T(8,128)S(1)} %concatenate.3), channel_id=1, source_target_pairs={{0,64},{64,128},{128,192},{1,65},{65,129},{129,193},{2,66},{66,130... | collective-permute-start | bytes 417800 | tf_op jit(solution)/shard_map/ppermute | solution.py:266
  26.5 0.1 dynamic_slice.3
  26.6 0.2 slice.16
  26.8 0.2 slice.15
  27.0 0.0 copy-done.5
  27.0 1.1 table.1
  28.2 6.8 %main.1 = (f32[16,128,256]{2,1,0:T(8,128)}, f32[16,128,128]{2,1,0:T(8,128)S(1)}, f32[16,128,128]{2,1,0:T(8,128)S(1)}, f32[128,128]{1,0:T(8,128)S(1)}) custom-call(s32[1]{0:T(128)} %bitcast.rank_x_ref.rank_ref, f32[1,128]{1,0:T(1,128)S(1)} %bitcast.16, f32[32,128]{1,0:T(8,128)S(1)} %get-tuple-element.20.x_row_ref, f32[32,128,256]{2,1,0:T(8,128)} %x_ref.3, ...), custom_call_target="tpu_custom_call" | custom-call | flops 805306368 | bytes 10485760 | tf_op jit(solution)/shard_map/main/pallas_call | solution.py:328
  35.0 0.0 collective-permute-done.4.three_ref
  35.0 0.0 collective-permute-done.3.two_ref
  35.0 0.0 collective-permute-done.2.one_ref
  35.0 0.8 carry.1
  35.8 13.3 %all-gather = f32[1024,128]{1,0:T(8,128)S(1)} all-gather(f32[128,128]{1,0:T(8,128)S(1)} %get-tuple-element.34), channel_id=2, replica_groups=mesh['gx'=4,'gy'=8,'gz'=8] {'gz'}, dimensions={0}, use_global_device_ids=true | all-gather | bytes 589824 | tf_op jit(solution)/shard_map/all_gather | solution.py:359
  49.2 4.6 %last.1 = (f32[16,128,128]{2,1,0:T(8,128)}, f32[1024,8,128]{2,1,0:T(8,128)}) custom-call(s32[1]{0:T(128)} %bitcast.2.rank_ref, f32[16]{0:T(128)S(1)} %copy-done.1, s32[512]{0:T(512)S(1)} %multiply_add_fusion.1.place_ref, f32[16,128,128]{2,1,0:T(8,128)S(1)} %get-tuple-element.28.dz_ref, f32[16,128,128]{2,1,0:T(8,128)S(1)} %get-tuple-element.29.cz_ref, ...), custom_call_target="tpu_custom_call" | custom-call | tf_op jit(solution)/shard_map/last/pallas_call | solution.py:368
  53.7 107.9 %all_to_all.5 = f32[64,16,8,128]{3,2,1,0:T(8,128)S(1)} all-to-all(f32[64,16,8,128]{3,2,1,0:T(8,128)} %bitcast.21), channel_id=1, replica_groups=mesh['gx'=4,'gy'=8,'gz'=8] {'gy','gz'}, dimensions={0} | all-to-all | bytes 8388608 | tf_op jit(solution)/shard_map/all_to_all | solution.py:379
  161.6 2.0 %copy.12 = f32[1,64,16,2,4,128]{5,4,3,2,1,0:T(4,128)} copy(f32[1,64,16,2,4,128]{5,4,3,2,1,0:T(4,128)S(1)} %bitcast.20) | data formatting | bytes 8388608
  (10 shorter events, 0.0 us)
Async XLA Ops:
  0.6 10.2 %copy-start = (f32[16,16]{1,0:T(8,128)S(1)}, f32[16,16]{1,0:T(8,128)}, u32[]{:S(2)}) copy-start(f32[16,16]{1,0:T(8,128)} %f_ref.2) | copy-start | bytes 3076
  0.6 10.2 %copy-start.2 = (f32[128]{0:T(128)S(1)}, f32[128]{0:T(128)}, u32[]{:S(2)}) copy-start(f32[128]{0:T(128)} %param.9) | copy-start | bytes 1540
  0.7 11.4 %copy-start.1 = (f32[16]{0:T(128)S(1)}, f32[16]{0:T(128)}, u32[]{:S(2)}) copy-start(f32[16]{0:T(128)} %g_ref.3) | copy-start | bytes 196
  0.7 12.5 %copy-start.6 = (s32[512,1]{0,1:T(1,128)S(1)}, s32[512,1]{0,1:T(1,128)}, u32[]{:S(2)}) copy-start(s32[512,1]{0,1:T(1,128)} %param.15) | copy-start | bytes 6148
  0.7 25.8 %copy-start.3 = (f32[2048]{0:T(1024)S(1)}, f32[2048]{0:T(1024)}, u32[]{:S(2)}) copy-start(f32[2048]{0:T(1024)} %h_ref.1) | copy-start | bytes 24580
  0.7 26.3 %copy-start.5 = (f32[128]{0:T(128)S(1)}, f32[128]{0:T(128)}, u32[]{:S(2)}) copy-start(f32[128]{0:T(128)} %param.14) | copy-start | bytes 1540
  0.7 26.3 %copy-start.4 = (f32[128,128]{1,0:T(8,128)S(1)}, f32[128,128]{1,0:T(8,128)}, u32[]{:S(2)}) copy-start(f32[128,128]{1,0:T(8,128)} %f_ref.3) | copy-start | bytes 196612
  5.0 8.4 %collective-permute-start = (f32[128,256]{1,0:T(8,128)}, f32[128,256]{1,0:T(8,128)S(1)}, u32[]{:S(2)}, u32[]{:S(2)}) collective-permute-start(f32[128,256]{1,0:T(8,128)} %get-tuple-element.21), channel_id=1, source_target_pairs={{64,0},{128,64},{192,128},{65,1},{129,65},{193,129},{66,2},{130,66... | collective-permute-start | bytes 393224 | tf_op jit(solution)/shard_map/ppermute | solution.py:266
  6.3 7.4 %collective-permute-start.1 = (f32[128,256]{1,0:T(8,128)}, f32[128,256]{1,0:T(8,128)S(1)}, u32[]{:S(2)}, u32[]{:S(2)}) collective-permute-start(f32[128,256]{1,0:T(8,128)} %get-tuple-element.22), channel_id=1, source_target_pairs={{0,64},{64,128},{128,192},{1,65},{65,129},{129,193},{2,66},{66,130... | collective-permute-start | bytes 393224 | tf_op jit(solution)/shard_map/ppermute | solution.py:266
  16.6 18.4 %collective-permute-start.4 = (f32[136,256]{1,0:T(8,128)S(1)}, f32[136,256]{1,0:T(8,128)S(1)}, u32[]{:S(2)}, u32[]{:S(2)}) collective-permute-start(f32[136,256]{1,0:T(8,128)S(1)} %concatenate.3), channel_id=1, source_target_pairs={{0,192},{1,193},{2,194},{3,195},{4,196},{5,197},{6,198},{7,199},{8... | collective-permute-start | bytes 417800 | tf_op jit(solution)/shard_map/ppermute | solution.py:266
  22.4 12.6 %collective-permute-start.3 = (f32[136,256]{1,0:T(8,128)S(1)}, f32[136,256]{1,0:T(8,128)S(1)}, u32[]{:S(2)}, u32[]{:S(2)}) collective-permute-start(f32[136,256]{1,0:T(8,128)S(1)} %concatenate.3), channel_id=1, source_target_pairs={{0,128},{64,192},{1,129},{65,193},{2,130},{66,194},{3,131},{67,195... | collective-permute-start | bytes 417800 | tf_op jit(solution)/shard_map/ppermute | solution.py:266
  23.7 11.3 %collective-permute-start.2 = (f32[136,256]{1,0:T(8,128)S(1)}, f32[136,256]{1,0:T(8,128)S(1)}, u32[]{:S(2)}, u32[]{:S(2)}) collective-permute-start(f32[136,256]{1,0:T(8,128)S(1)} %concatenate.3), channel_id=1, source_target_pairs={{0,64},{64,128},{128,192},{1,65},{65,129},{129,193},{2,66},{66,130... | collective-permute-start | bytes 417800 | tf_op jit(solution)/shard_map/ppermute | solution.py:266

commit v6 on v5

--- a/solution.py
+++ b/solution.py
@@ -120,7 +120,7 @@
     row_ref[7:8] = jnp.zeros((1, 128), F32)
 
 
-def table_x_kernel(rank_x_ref, hx_ref, fx_ref, x_high_ref, x_low_ref, x_row_ref):
+def table_x_kernel(rank_x_ref, g_ref, hx_ref, fx_ref, x_high_ref, x_low_ref, x_row_ref, end_ref):
     base = rank_x_ref[0] * 32
     node = lax.broadcasted_iota(jnp.int32, (128, 128), 0)
     place = lax.broadcasted_iota(jnp.int32, (128, 128), 1)
@@ -149,6 +149,9 @@
     x_high_ref[...], x_low_ref[...] = high, low
     x_row_ref[0:16, :] = jnp.broadcast_to(factor[:, 15:16] * (-near[:, 15:16] * b[:, 15:16]), (16, 128))
     x_row_ref[16:32, :] = jnp.broadcast_to(factor[:, 0:1] * far_before, (16, 128))
+    end_ref[0:8, :] = jnp.broadcast_to(x_row_ref[15:16, 0:1], (8, 256))
+    end_ref[8:16, :] = jnp.broadcast_to(x_row_ref[31:32, 0:1], (8, 256))
+    end_ref[16:24, :] = jnp.full((8, 256), g_ref[15], F32)
 
 
 def dot3_left(high, low, value):
@@ -298,18 +301,20 @@
     near_space = lax.dynamic_slice_in_dim(spacing_z, rank_z[0] * 256, 256)
     square = jax.ShapeDtypeStruct((256, 256), BF16)
     oblong = jax.ShapeDtypeStruct((128, 256), BF16)
-    x_high, x_low, x_rows = pl.pallas_call(
+    x_high, x_low, x_rows, ends = pl.pallas_call(
         table_x_kernel,
-        in_specs=[s, v, v],
-        out_specs=[v] * 3,
-        out_shape=[oblong, oblong, jax.ShapeDtypeStruct((32, 128), F32)],
+        in_specs=[s, s, v, v],
+        out_specs=[v] * 4,
+        out_shape=[
+            oblong, oblong, jax.ShapeDtypeStruct((32, 128), F32), jax.ShapeDtypeStruct((24, 256), F32),
+        ],
         compiler_params=params(),
         cost_estimate=cost(1 << 22, 1 << 17),
         name="table_x",
-    )(rank_x, space_x, operator_x)
-
-    total = own + x_rows[15:16, 0:1] * right + x_rows[31:32, 0:1] * left
-    ended = jnp.concatenate([total, jnp.broadcast_to(persist_x[15], (8, 256))], axis=0)
+    )(rank_x, persist_x, space_x, operator_x)
+
+    total = own + ends[0:1] * right + ends[8:9] * left
+    ended = jnp.concatenate([total, ends[16:24]], axis=0)
     one, two, three = (shift(ended, "gx", by) for by in (1, 2, 3))
 
     high, low, rows = pl.pallas_call(

time: 164 us -> 162 us (0.988)
  local copies, waits for them, and re-layouts: 4.27 us -> 2.57 us
  transfers between devices with their start and end apart: 5 -> 5, of which waited for: 1 -> 1; matrix products, arithmetic and copies ran while one was open for 1% -> 0% of each run, Pallas kernels for 6% -> 6%
where the time goes in v6:
time: 162 us
  blocking collectives  121 us (75%)
  Pallas kernels  19.3 us (12%)
  starting transfers between devices  15.7 us (10%)
  local copies, waits for them, and re-layouts  2.57 us (2%)
    all_to_all x1, blocking collectives, local(): lax.all_to_all(outgoing.reshape(group, capacity, 8, 128), ('gy', 'gz'), s...  108 us
    ppermute x5, starting transfers between devices, shift(): lax.ppermute(value, axis, [(i, i + by) for i in range(count) if 0 <= i +...  15.7 us
    all_gather x1, blocking collectives, local(): gathered = lax.all_gather(message, 'gz')  13.3 us
    pallas_call x1, Pallas kernels, local(): pl.pallas_call(main_kernel, grid=grid, in_specs=[s, whole((1, 128)), whol...  6.81 us
    pallas_call x1, Pallas kernels, local(): pl.pallas_call(last_kernel, in_specs=[s, s, s, v, v, v, v, v], out_specs=...  4.56 us
    pallas_call x1, Pallas kernels, local(): pl.pallas_call(head_kernel, grid=grid, in_specs=[s, s, whole((1, 128)), n...  4.32 us
  transfers between devices with their start and end apart: 5, of which 1 were waited for; matrix products, arithmetic and copies ran while one was open for 0% of the time, Pallas kernels for 6%

profile of v6, /device:TPU:8, one launch (start us, length us, event | category | flops | bytes accessed | tf_op | source)
XLA Modules:
  0.0 161.7 jit_solution(11913260763174994971)
XLA Ops:
  0.6 0.0 copy-start
  0.6 0.0 copy-start.2
  0.7 0.0 copy-start.1
  0.7 0.0 copy-start.6
  0.7 0.0 copy-start.3
  0.7 0.0 copy-start.5
  0.7 4.3 %head.1 = (f32[128,256]{1,0:T(8,128)}, f32[128,256]{1,0:T(8,128)}, f32[128,256]{1,0:T(8,128)}) custom-call(s32[1]{0:T(128)} %bitcast.rank_x_ref.rank_ref, f32[16,16]{1,0:T(8,128)} %f_ref.2, f32[1,128]{1,0:T(1,128)} %bitcast.13, f32[32,128,256]{2,1,0:T(8,128)} %x_ref.3), custom_call_target="tpu_custom_call" | custom-call | flops 2097152 | bytes 4194304 | tf_op jit(solution)/shard_map/head/pallas_call | solution.py:288
  5.0 1.3 collective-permute-start
  6.3 4.6 %collective-permute-start.1 = (f32[128,256]{1,0:T(8,128)}, f32[128,256]{1,0:T(8,128)S(1)}, u32[]{:S(2)}, u32[]{:S(2)}) collective-permute-start(f32[128,256]{1,0:T(8,128)} %get-tuple-element.23), channel_id=1, source_target_pairs={{0,64},{64,128},{128,192},{1,65},{65,129},{129,193},{2,66},{66,130... | collective-permute-start | bytes 393224 | tf_op jit(solution)/shard_map/ppermute | solution.py:269
  10.9 1.7 %table_x.1 = (bf16[128,256]{1,0:T(8,128)(2,1)S(1)}, bf16[128,256]{1,0:T(8,128)(2,1)S(1)}, f32[32,128]{1,0:T(8,128)S(1)}, f32[24,256]{1,0:T(8,128)S(1)}) custom-call(s32[1]{0:T(128)} %bitcast.rank_x_ref.rank_ref, f32[16]{0:T(128)S(1)} %copy-done.1, f32[1,128]{1,0:T(1,128)S(1)} %bitcast.14, f32[16,16]{1,0:T(8,128)S(1)} %copy-done), custom_call_target="tpu_custom_call" | custom-call | flops 4194304 | bytes 131072 | tf_op jit(solution)/shard_map/table_x/pallas_call | solution.py:304
  12.6 0.0 copy-done.6
  12.6 0.2 convert_reduce_fusion
  12.9 0.0 collective-permute-done.right_ref
  12.9 0.8 collective-permute-done.1.left_ref
  13.7 0.9 multiply_add_fusion
  14.6 5.8 %collective-permute-start.4 = (f32[136,256]{1,0:T(8,128)S(1)}, f32[136,256]{1,0:T(8,128)S(1)}, u32[]{:S(2)}, u32[]{:S(2)}) collective-permute-start(f32[136,256]{1,0:T(8,128)S(1)} %pad_maximum_fusion), channel_id=1, source_target_pairs={{0,192},{1,193},{2,194},{3,195},{4,196},{5,197},{6,198},{7,199},{8... | collective-permute-start | bytes 417800 | tf_op jit(solution)/shard_map/ppermute | solution.py:269
  20.5 1.3 collective-permute-start.3
  21.8 2.8 %collective-permute-start.2 = (f32[136,256]{1,0:T(8,128)S(1)}, f32[136,256]{1,0:T(8,128)S(1)}, u32[]{:S(2)}, u32[]{:S(2)}) collective-permute-start(f32[136,256]{1,0:T(8,128)S(1)} %pad_maximum_fusion), channel_id=1, source_target_pairs={{0,64},{64,128},{128,192},{1,65},{65,129},{129,193},{2,66},{66,130... | collective-permute-start | bytes 417800 | tf_op jit(solution)/shard_map/ppermute | solution.py:269
  24.6 0.1 dynamic_slice.3
  24.7 0.2 slice.16
  24.9 0.2 slice.15
  25.1 0.0 copy-done.5
  25.1 1.1 table.1
  26.2 6.8 %main.1 = (f32[16,128,256]{2,1,0:T(8,128)}, f32[16,128,128]{2,1,0:T(8,128)S(1)}, f32[16,128,128]{2,1,0:T(8,128)S(1)}, f32[128,128]{1,0:T(8,128)S(1)}) custom-call(s32[1]{0:T(128)} %bitcast.rank_x_ref.rank_ref, f32[1,128]{1,0:T(1,128)S(1)} %bitcast.15, f32[32,128]{1,0:T(8,128)S(1)} %get-tuple-element.21.x_row_ref, f32[32,128,256]{2,1,0:T(8,128)} %x_ref.3, ...), custom_call_target="tpu_custom_call" | custom-call | flops 805306368 | bytes 10485760 | tf_op jit(solution)/shard_map/main/pallas_call | solution.py:333
  33.0 0.0 collective-permute-done.4.three_ref
  33.1 0.0 collective-permute-done.3.two_ref
  33.1 0.0 collective-permute-done.2.one_ref
  33.1 0.8 carry.1
  33.9 13.3 %all-gather = f32[1024,128]{1,0:T(8,128)S(1)} all-gather(f32[128,128]{1,0:T(8,128)S(1)} %get-tuple-element.36), channel_id=2, replica_groups=mesh['gx'=4,'gy'=8,'gz'=8] {'gz'}, dimensions={0}, use_global_device_ids=true | all-gather | bytes 589824 | tf_op jit(solution)/shard_map/all_gather | solution.py:364
  47.3 4.6 %last.1 = (f32[16,128,128]{2,1,0:T(8,128)}, f32[1024,8,128]{2,1,0:T(8,128)}) custom-call(s32[1]{0:T(128)} %bitcast.2.rank_ref, f32[16]{0:T(128)S(1)} %copy-done.1, s32[512]{0:T(512)S(1)} %multiply_add_fusion.1.place_ref, f32[16,128,128]{2,1,0:T(8,128)S(1)} %get-tuple-element.29.dz_ref, f32[16,128,128]{2,1,0:T(8,128)S(1)} %get-tuple-element.30.cz_ref, ...), custom_call_target="tpu_custom_call" | custom-call | tf_op jit(solution)/shard_map/last/pallas_call | solution.py:373
  51.8 107.9 %all_to_all.5 = f32[64,16,8,128]{3,2,1,0:T(8,128)S(1)} all-to-all(f32[64,16,8,128]{3,2,1,0:T(8,128)} %bitcast.20), channel_id=1, replica_groups=mesh['gx'=4,'gy'=8,'gz'=8] {'gy','gz'}, dimensions={0} | all-to-all | bytes 8388608 | tf_op jit(solution)/shard_map/all_to_all | solution.py:384
  159.7 2.0 %copy.12 = f32[1,64,16,2,4,128]{5,4,3,2,1,0:T(4,128)} copy(f32[1,64,16,2,4,128]{5,4,3,2,1,0:T(4,128)S(1)} %bitcast.19) | data formatting | bytes 8388608
  (10 shorter events, 0.0 us)
Async XLA Ops:
  0.6 10.2 %copy-start = (f32[16,16]{1,0:T(8,128)S(1)}, f32[16,16]{1,0:T(8,128)}, u32[]{:S(2)}) copy-start(f32[16,16]{1,0:T(8,128)} %f_ref.2) | copy-start | bytes 3076
  0.6 10.2 %copy-start.2 = (f32[128]{0:T(128)S(1)}, f32[128]{0:T(128)}, u32[]{:S(2)}) copy-start(f32[128]{0:T(128)} %param.9) | copy-start | bytes 1540
  0.7 10.2 %copy-start.1 = (f32[16]{0:T(128)S(1)}, f32[16]{0:T(128)}, u32[]{:S(2)}) copy-start(f32[16]{0:T(128)} %g_ref.5) | copy-start | bytes 196
  0.7 12.0 %copy-start.6 = (s32[512,1]{0,1:T(1,128)S(1)}, s32[512,1]{0,1:T(1,128)}, u32[]{:S(2)}) copy-start(s32[512,1]{0,1:T(1,128)} %param.15) | copy-start | bytes 6148
  0.7 23.9 %copy-start.3 = (f32[2048]{0:T(1024)S(1)}, f32[2048]{0:T(1024)}, u32[]{:S(2)}) copy-start(f32[2048]{0:T(1024)} %h_ref.1) | copy-start | bytes 24580
  0.7 24.4 %copy-start.5 = (f32[128]{0:T(128)S(1)}, f32[128]{0:T(128)}, u32[]{:S(2)}) copy-start(f32[128]{0:T(128)} %param.14) | copy-start | bytes 1540
  0.7 24.4 %copy-start.4 = (f32[128,128]{1,0:T(8,128)S(1)}, f32[128,128]{1,0:T(8,128)}, u32[]{:S(2)}) copy-start(f32[128,128]{1,0:T(8,128)} %f_ref.3) | copy-start | bytes 196612
  5.0 7.9 %collective-permute-start = (f32[128,256]{1,0:T(8,128)}, f32[128,256]{1,0:T(8,128)S(1)}, u32[]{:S(2)}, u32[]{:S(2)}) collective-permute-start(f32[128,256]{1,0:T(8,128)} %get-tuple-element.22), channel_id=1, source_target_pairs={{64,0},{128,64},{192,128},{65,1},{129,65},{193,129},{66,2},{130,66... | collective-permute-start | bytes 393224 | tf_op jit(solution)/shard_map/ppermute | solution.py:269
  6.3 7.4 %collective-permute-start.1 = (f32[128,256]{1,0:T(8,128)}, f32[128,256]{1,0:T(8,128)S(1)}, u32[]{:S(2)}, u32[]{:S(2)}) collective-permute-start(f32[128,256]{1,0:T(8,128)} %get-tuple-element.23), channel_id=1, source_target_pairs={{0,64},{64,128},{128,192},{1,65},{65,129},{129,193},{2,66},{66,130... | collective-permute-start | bytes 393224 | tf_op jit(solution)/shard_map/ppermute | solution.py:269
  14.6 18.4 %collective-permute-start.4 = (f32[136,256]{1,0:T(8,128)S(1)}, f32[136,256]{1,0:T(8,128)S(1)}, u32[]{:S(2)}, u32[]{:S(2)}) collective-permute-start(f32[136,256]{1,0:T(8,128)S(1)} %pad_maximum_fusion), channel_id=1, source_target_pairs={{0,192},{1,193},{2,194},{3,195},{4,196},{5,197},{6,198},{7,199},{8... | collective-permute-start | bytes 417800 | tf_op jit(solution)/shard_map/ppermute | solution.py:269
  20.5 12.6 %collective-permute-start.3 = (f32[136,256]{1,0:T(8,128)S(1)}, f32[136,256]{1,0:T(8,128)S(1)}, u32[]{:S(2)}, u32[]{:S(2)}) collective-permute-start(f32[136,256]{1,0:T(8,128)S(1)} %pad_maximum_fusion), channel_id=1, source_target_pairs={{0,128},{64,192},{1,129},{65,193},{2,130},{66,194},{3,131},{67,195... | collective-permute-start | bytes 417800 | tf_op jit(solution)/shard_map/ppermute | solution.py:269
  21.8 11.3 %collective-permute-start.2 = (f32[136,256]{1,0:T(8,128)S(1)}, f32[136,256]{1,0:T(8,128)S(1)}, u32[]{:S(2)}, u32[]{:S(2)}) collective-permute-start(f32[136,256]{1,0:T(8,128)S(1)} %pad_maximum_fusion), channel_id=1, source_target_pairs={{0,64},{64,128},{128,192},{1,65},{65,129},{129,193},{2,66},{66,130... | collective-permute-start | bytes 417800 | tf_op jit(solution)/shard_map/ppermute | solution.py:269
